TPU v7x, 32 devices: a whole 2x2x4 slice. The times are simulated.
32 devices in a mesh: box: 8 (over z, y), op: 4 (over x, core).
Axes of the slice: x: 2, y: 2, z: 4, core: 2. Of those that a mesh axis runs over, the one named last changes fastest.
Arguments:
- density: float32 [2304, 296], P(('box', 'op')), may hold values from -6 to 6
- operators: float32 [64, 296, 296], P('op'), may hold values from -0.046875 to 0.046875
- owner_count: int32 [8], replicated, may hold values from 96 to 288, as said below
- group_count: int32 [8], replicated, may hold values from 96 to 288, as said below
- target_slot: int32 [8, 64, 288], P('box', 'op'), may hold values from 0 to 288, as said below
- source_box: int32 [8, 64, 288], P('box', 'op'), may hold values from 0 to 1535, as said below
Outputs:
- check_potential: float32 [2304, 296], P(('box', 'op'))
Inputs may be any that keep to these rules, and one draw needn't show every extreme that they name: `owner_count`: the counts sum to 1536. The start of owner d and the start of group d (sums of earlier counts) lie within 48 of d * 192, so they differ by at most 96, and some owner holds exactly 288 boxes. `group_count`: the counts sum to 1536, starts as for owner_count; some group holds exactly 288 boxes, and in every draw some group start lies 96 above the owner start of the same index. `target_slot`: entry j of a list of group g holds j or 288; where it holds j, j is below group_count[g]. `source_box`: an entry of group g's lists lies between group_start[g] - 96 and group_start[g + 1] + 96 - 1 (group_start[8] = 1536).
All inputs are finite; a program needn't handle non-finite values.
Results may differ from a plain program's by a relative error of at most 0.0001.
Values sent between devices are 32-bit elements; how exact they have to be, the bound alone decides.
No kernel may reach another device: no remote copies, remote signals or barrier semaphores. Data moves between devices by JAX's collectives and lax.ppermute only.
A program may use at most 64 MiB of HBM per device.

v0:
```python
import jax
import jax.numpy as jnp
from jax import lax
from jax.sharding import PartitionSpec as P


def extended(block, sides, width):
    for axis, dim in sides:
        count = lax.axis_size(axis)
        forward = [(i, i + 1) for i in range(count - 1)]
        backward = [(target, source) for source, target in forward]
        low = lax.ppermute(
            lax.slice_in_dim(block, block.shape[dim] - width, None, axis=dim), axis, forward
        )
        high = lax.ppermute(lax.slice_in_dim(block, 0, width, axis=dim), axis, backward)
        block = jnp.concatenate([low, block, high], axis=dim)
    return block


def exclusive_starts(counts):
    running = jnp.cumsum(counts, dtype=jnp.int32)
    return jnp.concatenate([jnp.zeros((1,), jnp.int32), running])


def neighbours(block_rows, capacity):
    return extended(block_rows, (("box", 0),), capacity)


def window_ids(morton, starts, box_index, capacity):
    this_start = starts[box_index]
    later_start = starts[box_index + 1]
    earlier_start = starts[jnp.maximum(box_index - 1, 0)]
    found = jnp.where(
        morton < this_start,
        morton - earlier_start,
        jnp.where(
            morton < later_start,
            capacity + morton - this_start,
            2 * capacity + morton - later_start,
        ),
    )
    window_len = 3 * capacity
    return jnp.clip(found, 0, window_len - 1)


def relocate(block_rows, from_starts, to_start, to_count, box_index, capacity):
    window = neighbours(block_rows, capacity)
    slot_ids = jnp.arange(capacity, dtype=jnp.int32)
    found = window_ids(to_start + slot_ids, from_starts, box_index, capacity)
    moved_rows = window[found]
    return jnp.where((slot_ids < to_count)[:, None], moved_rows, 0.0)


def body(density, operators, owner_count, group_count, target_slot, source_box):
    quarter = density.shape[0]
    capacity = quarter * lax.axis_size("op")
    box_index = lax.axis_index("box")
    owner_starts = exclusive_starts(owner_count)
    group_starts = exclusive_starts(group_count)
    owned_rows = lax.all_gather(density, "op", axis=0, tiled=True)
    grouped = relocate(
        owned_rows,
        owner_starts,
        group_starts[box_index],
        group_count[box_index],
        box_index,
        capacity,
    )
    window = neighbours(grouped, capacity)
    source_ids = window_ids(source_box[0].T, group_starts, box_index, capacity)
    live_mask = (target_slot[0].T < capacity)[:, :, None]
    source_rows = jnp.where(live_mask, window[source_ids], 0.0)
    partial_value = jnp.einsum(
        "jkl,kil->ji", source_rows, operators, precision=lax.Precision.HIGHEST
    )
    column_part = lax.psum_scatter(partial_value, "op", scatter_dimension=1, tiled=True)
    returned = relocate(
        column_part,
        group_starts,
        owner_starts[box_index],
        owner_count[box_index],
        box_index,
        capacity,
    )
    return lax.all_to_all(returned, "op", split_axis=0, concat_axis=1, tiled=True)


def solution(mesh):
    placed = (
        P(("box", "op"), None),
        P("op", None, None),
        P(),
        P(),
        P("box", "op", None),
        P("box", "op", None),
    )
    return jax.shard_map(
        body, mesh=mesh, in_specs=placed, out_specs=P(("box", "op"), None), check_vma=False
    )
```

profile of v0, /device:TPU:0, one launch (start us, length us, event | category | flops | bytes accessed | tf_op | source)
XLA Modules:
  0.0 126.8 jit_solution(10534544947407263361)
XLA Ops:
  0.0 8.4 %all_gather.3 = f32[288,296]{1,0:T(8,128)S(1)} all-gather(f32[72,296]{1,0:T(8,128)} %param.6), channel_id=1, replica_groups=mesh['box'=8,'op'=4] {'op'}, dimensions={0}, use_global_device_ids=true | all-gather | bytes 426240 | tf_op jit(solution)/shard_map/all_gather | solution.py:60
  8.4 3.4 %collective-permute-start = (f32[288,296]{1,0:T(8,128)S(1)}, f32[288,296]{1,0:T(8,128)S(1)}, u32[]{:S(2)}, u32[]{:S(2)}) collective-permute-start(f32[288,296]{1,0:T(8,128)S(1)} %all_gather.3), channel_id=1, source_target_pairs={{0,4},{4,8},{8,12},{12,16},{16,20},{20,24},{24,28},{1,5},{5,9},{9,... | collective-permute-start | bytes 1022984 | tf_op jit(solution)/shard_map/ppermute | solution.py:12
  11.8 1.3 %collective-permute-start.1 = (f32[288,296]{1,0:T(8,128)S(1)}, f32[288,296]{1,0:T(8,128)S(1)}, u32[]{:S(2)}, u32[]{:S(2)}) collective-permute-start(f32[288,296]{1,0:T(8,128)S(1)} %all_gather.3), channel_id=1, source_target_pairs={{4,0},{8,4},{12,8},{16,12},{20,16},{24,20},{28,24},{5,1},{9,5},{13... | collective-permute-start | bytes 1022984 | tf_op jit(solution)/shard_map/ppermute | solution.py:15
  13.2 0.8 reduce-window.18
  14.0 0.8 reduce-window.19
  14.8 1.3 %dynamic_slice.30 = s32[1]{0:T(128)} dynamic-slice(s32[8]{0:T(128)} %param.9, s32[]{:T(128)S(6)} %select_n.110), dynamic_slice_sizes={1} | dynamic-slice | bytes 12 | tf_op jit(solution)/shard_map/dynamic_slice | solution.py:65
  16.2 0.7 fusion.10
  16.9 0.6 fusion.11
  17.5 2.5 %fusion.5 = s32[288]{0:T(512)S(1)} fusion(s32[]{:T(128)} %bitcast.11, s32[]{:T(128)} %bitcast.10, s32[]{:T(128)} %bitcast.9, s32[]{:T(128)} %bitcast.6), kind=kLoop, calls=%fused_computation.27 | loop fusion | flops 4032 | bytes 1168 | tf_op jit(solution)/shard_map/select_n | solution.py:50
  20.0 0.6 iota_compare_fusion
  20.7 10.5 %collective-permute-done = f32[288,296]{1,0:T(8,128)S(1)} collective-permute-done((f32[288,296]{1,0:T(8,128)S(1)}, f32[288,296]{1,0:T(8,128)S(1)}, u32[]{:S(2)}, u32[]{:S(2)}) %collective-permute-start) | collective-permute-done | bytes 341024 | tf_op jit(solution)/shard_map/ppermute | solution.py:12
  31.3 1.7 %gather_fusion = f32[288,296]{1,0:T(8,128)S(1)} fusion(f32[864,296]{1,0:T(8,128)S(1)} %pad_maximum_fusion, s32[1024]{0:T(1024)S(1)} %pad_clamp_fusion.2), kind=kCustom, calls=%fused_computation | custom fusion | bytes 683136 | tf_op jit(solution)/shard_map/gather | solution.py:50
  33.1 4.4 %collective-permute-start.2 = (f32[288,296]{1,0:T(8,128)S(1)}, f32[288,296]{1,0:T(8,128)S(1)}, u32[]{:S(2)}, u32[]{:S(2)}) collective-permute-start(f32[288,296]{1,0:T(8,128)S(1)} %broadcast_select_fusion), channel_id=1, source_target_pairs={{0,4},{4,8},{8,12},{12,16},{16,20},{20,24},{24,28},{1,5},{5,9},{9,... | collective-permute-start | bytes 1022984 | tf_op jit(solution)/shard_map/ppermute | solution.py:12
  37.6 1.3 %collective-permute-start.3 = (f32[288,296]{1,0:T(8,128)S(1)}, f32[288,296]{1,0:T(8,128)S(1)}, u32[]{:S(2)}, u32[]{:S(2)}) collective-permute-start(f32[288,296]{1,0:T(8,128)S(1)} %broadcast_select_fusion), channel_id=1, source_target_pairs={{4,0},{8,4},{12,8},{16,12},{20,16},{24,20},{28,24},{5,1},{9,5},{13... | collective-permute-start | bytes 1022984 | tf_op jit(solution)/shard_map/ppermute | solution.py:15
  38.9 1.9 %compare_select_fusion = s32[288,16]{0,1:T(8,128)S(1)} fusion(s32[1,16,288]{2,1,0:T(8,128)S(1)} %copy-done, s32[]{:T(128)} %bitcast.13, s32[]{:T(128)} %bitcast.12, s32[]{:T(128)} %bitcast.6), kind=kLoop, calls=%fused_computation.13 | loop fusion | flops 59904 | bytes 36876 | tf_op jit(solution)/shard_map/select_n | solution.py:72
  41.0 2.6 %fusion.6 = s32[288]{0:T(512)S(1)} fusion(s32[]{:T(128)} %bitcast.13, s32[]{:T(128)} %bitcast.12, s32[]{:T(128)} %bitcast.9, s32[]{:T(128)} %bitcast.6), kind=kLoop, calls=%fused_computation.28 | loop fusion | flops 4032 | bytes 1168 | tf_op jit(solution)/shard_map/select_n | solution.py:50
  43.6 12.5 %collective-permute-done.2 = f32[288,296]{1,0:T(8,128)S(1)} collective-permute-done((f32[288,296]{1,0:T(8,128)S(1)}, f32[288,296]{1,0:T(8,128)S(1)}, u32[]{:S(2)}, u32[]{:S(2)}) %collective-permute-start.2) | collective-permute-done | bytes 341024 | tf_op jit(solution)/shard_map/ppermute | solution.py:12
  56.2 12.2 %gather_fusion.1 = f32[4608,296]{1,0:T(8,128)} fusion(f32[864,296]{1,0:T(8,128)S(1)} %pad_maximum_fusion.1, s32[5120]{0:T(1024)S(1)} %pad_clamp_fusion), kind=kCustom, calls=%fused_computation.1 | custom fusion | bytes 10930176 | tf_op jit(solution)/shard_map/gather | solution.py:72
  68.4 19.9 %fusion.4 = f32[288,296]{0,1:T(8,128)S(1)} fusion(f32[16,296,296]{2,1,0:T(8,128)} %param.7, f32[288,16,296]{2,1,0:T(8,128)} %bitcast.29, pred[288,16]{0,1:T(8,128)(4,1)S(1)} %compare_bitcast_fusion), kind=kOutput, calls=%fused_computation.9 | convolution fusion | flops 4846178304 | bytes 11408896 | tf_op jit(solution)/shard_map/jkl,kil->ji/dot_general | solution.py:73
  88.3 10.1 %fusion = f32[288,80]{0,1:T(8,128)S(1)} fusion(f32[288,296]{0,1:T(8,128)S(1)} %fusion.4), kind=kCustom, calls=%all-reduce-scatter | all-reduce-scatter fusion | flops 92161 | bytes 433664
  98.4 1.3 %collective-permute-start.6 = (f32[288,18]{0,1:T(8,128)S(1)}, f32[288,18]{0,1:T(8,128)S(1)}, u32[]{:S(2)}, u32[]{:S(2)}) collective-permute-start(f32[288,18]{0,1:T(8,128)S(1)} %slice.6), channel_id=1, source_target_pairs={{0,1},{1,2},{2,3},{4,5},{5,6},{6,7},{8,9},{9,10},{10,11},{12,13},{... | collective-permute-start | bytes 62216
  99.7 0.7 dynamic_slice.29
  100.4 0.6 dynamic-slice.4
  101.6 0.3 concatenate.20
  102.0 4.4 %collective-permute-start.4 = (f32[288,74]{1,0:T(8,128)S(1)}, f32[288,74]{1,0:T(8,128)S(1)}, u32[]{:S(2)}, u32[]{:S(2)}) collective-permute-start(f32[288,74]{1,0:T(8,128)S(1)} %copy.16), channel_id=1, source_target_pairs={{0,4},{4,8},{8,12},{12,16},{16,20},{20,24},{24,28},{1,5},{5,9},{9,... | collective-permute-start | bytes 255752 | tf_op jit(solution)/shard_map/ppermute | solution.py:12
  106.4 1.3 %collective-permute-start.5 = (f32[288,74]{1,0:T(8,128)S(1)}, f32[288,74]{1,0:T(8,128)S(1)}, u32[]{:S(2)}, u32[]{:S(2)}) collective-permute-start(f32[288,74]{1,0:T(8,128)S(1)} %copy.16), channel_id=1, source_target_pairs={{4,0},{8,4},{12,8},{16,12},{20,16},{24,20},{28,24},{5,1},{9,5},{13... | collective-permute-start | bytes 255752 | tf_op jit(solution)/shard_map/ppermute | solution.py:15
  107.7 0.7 add_compare_fusion
  108.4 1.5 %collective-permute-done.4 = f32[288,74]{1,0:T(8,128)S(1)} collective-permute-done((f32[288,74]{1,0:T(8,128)S(1)}, f32[288,74]{1,0:T(8,128)S(1)}, u32[]{:S(2)}, u32[]{:S(2)}) %collective-permute-start.4) | collective-permute-done | bytes 85280 | tf_op jit(solution)/shard_map/ppermute | solution.py:12
  109.9 6.6 %collective-permute-done.5 = f32[288,74]{1,0:T(8,128)S(1)} collective-permute-done((f32[288,74]{1,0:T(8,128)S(1)}, f32[288,74]{1,0:T(8,128)S(1)}, u32[]{:S(2)}, u32[]{:S(2)}) %collective-permute-start.5) | collective-permute-done | bytes 85280 | tf_op jit(solution)/shard_map/ppermute | solution.py:15
  116.6 1.1 gather_fusion.2
  117.8 8.2 %all_to_all.16 = f32[4,72,74]{2,1,0:T(8,128)S(1)} all-to-all(f32[4,72,74]{2,1,0:T(8,128)S(1)} %broadcast_select_fusion.1), channel_id=1, replica_groups=mesh['box'=8,'op'=4] {'op'}, dimensions={0} | all-to-all | bytes 170496 | tf_op jit(solution)/shard_map/all_to_all | solution.py:85
  126.0 0.8 all_to_all.14
  (27 shorter events, 0.9 us)
Async XLA Ops:
  8.4 22.8 %collective-permute-start = (f32[288,296]{1,0:T(8,128)S(1)}, f32[288,296]{1,0:T(8,128)S(1)}, u32[]{:S(2)}, u32[]{:S(2)}) collective-permute-start(f32[288,296]{1,0:T(8,128)S(1)} %all_gather.3), channel_id=1, source_target_pairs={{0,4},{4,8},{8,12},{12,16},{16,20},{20,24},{24,28},{1,5},{5,9},{9,... | collective-permute-start | bytes 1022984 | tf_op jit(solution)/shard_map/ppermute | solution.py:12
  11.8 19.4 %collective-permute-start.1 = (f32[288,296]{1,0:T(8,128)S(1)}, f32[288,296]{1,0:T(8,128)S(1)}, u32[]{:S(2)}, u32[]{:S(2)}) collective-permute-start(f32[288,296]{1,0:T(8,128)S(1)} %all_gather.3), channel_id=1, source_target_pairs={{4,0},{8,4},{12,8},{16,12},{20,16},{24,20},{28,24},{5,1},{9,5},{13... | collective-permute-start | bytes 1022984 | tf_op jit(solution)/shard_map/ppermute | solution.py:15
  31.3 7.5 %copy-start = (s32[1,16,288]{2,1,0:T(8,128)S(1)}, s32[1,16,288]{2,1,0:T(8,128)}, u32[]{:S(2)}) copy-start(s32[1,16,288]{2,1,0:T(8,128)} %param.11) | copy-start | bytes 55300
  31.3 12.2 %copy-start.1 = (s32[1,16,288]{2,1,0:T(8,128)S(1)}, s32[1,16,288]{2,1,0:T(8,128)}, u32[]{:S(2)}) copy-start(s32[1,16,288]{2,1,0:T(8,128)} %param.10) | copy-start | bytes 55300
  33.1 22.9 %collective-permute-start.2 = (f32[288,296]{1,0:T(8,128)S(1)}, f32[288,296]{1,0:T(8,128)S(1)}, u32[]{:S(2)}, u32[]{:S(2)}) collective-permute-start(f32[288,296]{1,0:T(8,128)S(1)} %broadcast_select_fusion), channel_id=1, source_target_pairs={{0,4},{4,8},{8,12},{12,16},{16,20},{20,24},{24,28},{1,5},{5,9},{9,... | collective-permute-start | bytes 1022984 | tf_op jit(solution)/shard_map/ppermute | solution.py:12
  37.6 18.5 %collective-permute-start.3 = (f32[288,296]{1,0:T(8,128)S(1)}, f32[288,296]{1,0:T(8,128)S(1)}, u32[]{:S(2)}, u32[]{:S(2)}) collective-permute-start(f32[288,296]{1,0:T(8,128)S(1)} %broadcast_select_fusion), channel_id=1, source_target_pairs={{4,0},{8,4},{12,8},{16,12},{20,16},{24,20},{28,24},{5,1},{9,5},{13... | collective-permute-start | bytes 1022984 | tf_op jit(solution)/shard_map/ppermute | solution.py:15
  68.4 31.3 %copy-start.3 = (s32[8]{0:T(128)S(1)}, s32[8]{0:T(128)}, u32[]{:S(2)}) copy-start(s32[8]{0:T(128)} %param.8) | copy-start | bytes 100
  68.4 32.0 %copy-start.2 = (u32[32]{0:T(128)S(1)}, u32[32]{0:T(128)}, u32[]{:S(2)}) copy-start(u32[32]{0:T(128)} %constant.47) | copy-start | bytes 388
  98.4 3.2 %collective-permute-start.6 = (f32[288,18]{0,1:T(8,128)S(1)}, f32[288,18]{0,1:T(8,128)S(1)}, u32[]{:S(2)}, u32[]{:S(2)}) collective-permute-start(f32[288,18]{0,1:T(8,128)S(1)} %slice.6), channel_id=1, source_target_pairs={{0,1},{1,2},{2,3},{4,5},{5,6},{6,7},{8,9},{9,10},{10,11},{12,13},{... | collective-permute-start | bytes 62216
  102.0 7.9 %collective-permute-start.4 = (f32[288,74]{1,0:T(8,128)S(1)}, f32[288,74]{1,0:T(8,128)S(1)}, u32[]{:S(2)}, u32[]{:S(2)}) collective-permute-start(f32[288,74]{1,0:T(8,128)S(1)} %copy.16), channel_id=1, source_target_pairs={{0,4},{4,8},{8,12},{12,16},{16,20},{20,24},{24,28},{1,5},{5,9},{9,... | collective-permute-start | bytes 255752 | tf_op jit(solution)/shard_map/ppermute | solution.py:12
  106.4 10.1 %collective-permute-start.5 = (f32[288,74]{1,0:T(8,128)S(1)}, f32[288,74]{1,0:T(8,128)S(1)}, u32[]{:S(2)}, u32[]{:S(2)}) collective-permute-start(f32[288,74]{1,0:T(8,128)S(1)} %copy.16), channel_id=1, source_target_pairs={{4,0},{8,4},{12,8},{16,12},{20,16},{24,20},{28,24},{5,1},{9,5},{13... | collective-permute-start | bytes 255752 | tf_op jit(solution)/shard_map/ppermute | solution.py:15
where the time goes:
time: 128 us; the launch traced here: 127 us
  waiting for transfers between devices  31.2 us (24%)
  blocking collectives  26.6 us (21%)
  local copies, waits for them, and re-layouts  20.2 us (16%)
  matrix products  19.9 us (16%)
  starting transfers between devices  17.4 us (14%)
  other arithmetic  10.5 us (8%)
    ppermute x3, waiting for transfers between devices, extended(): lax.ppermute(lax.slice_in_dim(block, block.shape[dim] - width, None, axis...  24.5 us
    dot_general x1, matrix products, body(): jnp.einsum('jkl,kil->ji', source_rows, operators, precision=lax.Precision...  19.9 us
    ppermute x3, starting transfers between devices, extended(): lax.ppermute(lax.slice_in_dim(block, block.shape[dim] - width, None, axis...  12.2 us
    gather x1, local copies, waits for them, and re-layouts, body(): source_rows = jnp.where(live_mask, window[source_ids], 0.0)  12.2 us
    unnamed x1, blocking collectives  10.1 us
    all_gather x1, blocking collectives, body(): owned_rows = lax.all_gather(density, 'op', axis=0, tiled=True)  8.4 us
    all_to_all x1, blocking collectives, body(): lax.all_to_all(returned, 'op', split_axis=0, concat_axis=1, tiled=True)  8.18 us
    ppermute x3, waiting for transfers between devices, extended(): lax.ppermute(lax.slice_in_dim(block, 0, width, axis=dim), axis, backward)  6.64 us
  transfers between devices with their start and end apart: 7, of which 4 were waited for; matrix products, arithmetic and copies ran while one was open for 11% of the time, Pallas kernels for 0%

commit v1 on v0

v1 whole, which is shorter than its diff:
```python
import functools

import jax
import jax.numpy as jnp
from jax import lax
from jax.experimental import pallas as pl
from jax.experimental.pallas import tpu as pltpu
from jax.sharding import PartitionSpec as P

LANES = 128


def padded(size, to=LANES):
    return -(-size // to) * to


def shifted(pairs_axis, step):
    count = lax.axis_size(pairs_axis)
    return [(i, i + step) for i in range(count) if 0 <= i + step < count]


def flip(block, bit):
    count = lax.axis_size("op")
    return lax.ppermute(block, "op", [(i, i ^ bit) for i in range(count)])


def to_box(block, step):
    return lax.ppermute(block, "box", shifted("box", step))


def prefix(count_ref, upto):
    return lax.fori_loop(0, upto, lambda i, total: total + count_ref[i], 0)


def places(owner_ref, group_ref, box, boxes, capacity):
    before = jnp.maximum(box - 1, 0)
    after = jnp.minimum(box + 1, boxes - 1)
    own_start = prefix(owner_ref, box)
    own_count = owner_ref[box]
    prev_count = jnp.where(box > 0, owner_ref[before], 0)
    prev_start = own_start - jnp.where(box > 0, prev_count, capacity)
    next_start = own_start + own_count
    next_count = jnp.where(box < boxes - 1, owner_ref[after], 0)
    return (
        (prev_start, own_start, next_start),
        (prev_count, own_count, next_count),
        prefix(group_ref, box),
    )


def operator_kernel(op_ref, out_ref, *, size, whole):
    tail = size - whole
    block = op_ref[0]
    high = block.astype(jnp.bfloat16)
    low = block - high.astype(jnp.float32)
    out_ref[0, :, :whole] = high[:, :whole]
    out_ref[0, :, whole : 2 * whole] = low[:, :whole].astype(jnp.bfloat16)
    room = jnp.zeros((size, LANES - tail), jnp.float32)
    high_tail = jnp.concatenate([high[:, whole:].astype(jnp.float32), room], axis=1)
    low_tail = jnp.concatenate([low[:, whole:], room], axis=1)
    rest = high_tail + pltpu.roll(high_tail, tail, 1) + pltpu.roll(low_tail, 2 * tail, 1)
    out_ref[0, :, 2 * whole :] = rest.astype(jnp.bfloat16)


def split_operators(operators):
    count, size, _ = operators.shape
    whole = size // LANES * LANES
    width = 2 * whole + LANES
    return pl.pallas_call(
        functools.partial(operator_kernel, size=size, whole=whole),
        grid=(count,),
        in_specs=[pl.BlockSpec((1, size, size), lambda k: (k, 0, 0))],
        out_specs=pl.BlockSpec((1, size, width), lambda k: (k, 0, 0)),
        out_shape=jax.ShapeDtypeStruct((count, size, width), jnp.bfloat16),
        cost_estimate=pl.CostEstimate(
            flops=0, transcendentals=0, bytes_accessed=count * size * (4 * size + 2 * width)
        ),
        name="split_operators",
    )(operators)


def select_kernel(owner_ref, group_ref, target_ref, source_ref, out_ref, side_ref, *, boxes, capacity, quarter, span):
    box = lax.axis_index("box")
    core = lax.axis_index("op") % 2
    starts, _, group_start = places(owner_ref, group_ref, box, boxes, capacity)
    first = group_start - capacity // 3
    alive = target_ref[0] < capacity
    found = jnp.where(alive, source_ref[0] - first, -1)
    offsets = found.shape[0]
    found = jnp.concatenate(
        [found, jnp.full((offsets, padded(capacity) - capacity), -1, jnp.int32)], axis=1
    )
    columns = found.T
    row = lax.broadcasted_iota(jnp.int32, (capacity, span), 1)
    for k in range(offsets):
        hit = columns[:capacity, k : k + 1] == row
        out_ref[k] = jnp.where(hit, 1.0, 0.0).astype(jnp.bfloat16)
    tail = group_start + group_ref[box] - starts[1]
    slot = quarter * core + lax.broadcasted_iota(jnp.int32, side_ref.shape, 0)
    side_ref[...] = jnp.where(slot >= tail, 1.0, 0.0)


def selections(owner_count, group_count, target_slot, source_box, boxes, quarter, span):
    _, offsets, capacity = target_slot.shape
    smem = pl.BlockSpec(memory_space=pltpu.SMEM)
    vmem = pl.BlockSpec(memory_space=pltpu.VMEM)
    return pl.pallas_call(
        functools.partial(
            select_kernel, boxes=boxes, capacity=capacity, quarter=quarter, span=span
        ),
        in_specs=[smem, smem, vmem, vmem],
        out_specs=[vmem, vmem],
        out_shape=[
            jax.ShapeDtypeStruct((offsets, capacity, span), jnp.bfloat16),
            jax.ShapeDtypeStruct((quarter, LANES), jnp.float32),
        ],
        cost_estimate=pl.CostEstimate(
            flops=0, transcendentals=0, bytes_accessed=2 * offsets * capacity * span
        ),
        name="selections",
    )(owner_count, group_count, target_slot, source_box)


def translate_kernel(
    owner_ref,
    group_ref,
    own_ref,
    own_peer_ref,
    near_ref,
    near_peer_ref,
    weight_ref,
    pick_ref,
    send_ref,
    keep_ref,
    window,
    packed,
    total,
    *,
    boxes,
    capacity,
    quarter,
    size,
    span,
    need,
):
    step = pl.program_id(0)
    box = lax.axis_index("box")
    device = lax.axis_index("op")
    core = device % 2
    whole = size // LANES * LANES
    tail = size - whole
    third = capacity // 3
    tiles = padded(size) // LANES
    starts, counts, group_start = places(owner_ref, group_ref, box, boxes, capacity)

    def columns(tile):
        return slice(tile * LANES, min((tile + 1) * LANES, size))

    @pl.when(step == 0)
    def _():
        margin = 2 * third
        for tile in range(tiles):
            window[tile, margin + need : margin + span, :] = jnp.zeros((span - need, LANES), jnp.float32)
        for owner in range(3):
            for part in range(4):
                at = margin + starts[owner] + quarter * part - (group_start - third)
                at = jnp.clip(at, 0, window.shape[1] - quarter)
                mask = device ^ part
                line = pl.multiple_of(
                    jnp.where(mask >= 2, quarter * (1 if owner == 1 else 2), 0)
                    + (quarter if owner == 2 else 0),
                    8,
                )
                mine, peers = (own_ref, own_peer_ref) if owner == 1 else (near_ref, near_peer_ref)

                def put(source):
                    for tile in range(tiles):
                        lanes = columns(tile)
                        window[tile, pl.ds(at, quarter), : lanes.stop - lanes.start] = source[
                            pl.ds(line, quarter), lanes
                        ]

                pl.when(mask % 2 == 0)(functools.partial(put, mine))
                pl.when(mask % 2 == 1)(functools.partial(put, peers))
        for tile in range(tiles):
            value = window[tile, margin : margin + span, :]
            row = lax.broadcasted_iota(jnp.int32, value.shape, 0)
            lane = lax.broadcasted_iota(jnp.int32, value.shape, 1)
            fine = row < need
            if tile == tiles - 1:
                fine = fine & (lane < tail)
            value = jnp.where(fine, value, 0.0)
            high = value.astype(jnp.bfloat16)
            low = value - high.astype(jnp.float32)
            if tile < tiles - 1:
                packed[:, tile * LANES : (tile + 1) * LANES] = high
                packed[:, whole + tile * LANES : whole + (tile + 1) * LANES] = low.astype(jnp.bfloat16)
            else:
                high = high.astype(jnp.float32)
                rest = high + pltpu.roll(low, tail, 1) + pltpu.roll(high, 2 * tail, 1)
                packed[:, 2 * whole :] = rest.astype(jnp.bfloat16)
        total[...] = jnp.zeros(total.shape, jnp.float32)

    picked = jnp.dot(pick_ref[0], packed[...], preferred_element_type=jnp.float32).astype(jnp.bfloat16)
    weight = weight_ref[0]
    left = jnp.concatenate([picked[:, : 2 * whole], picked[:, :whole], picked[:, 2 * whole :]], axis=1)
    right = jnp.concatenate([weight[:, :whole], weight], axis=1)
    part = lax.dot_general(left, right, (((1,), (1,)), ((), ())), preferred_element_type=jnp.float32)
    for tile in range(tiles):
        lanes = columns(tile)
        total[tile, capacity : 2 * capacity, : lanes.stop - lanes.start] += part[:, lanes]

    @pl.when(step == pl.num_programs(0) - 1)
    def _():
        def rows(owner, block):
            at = capacity + starts[owner] - group_start + quarter * block
            at = jnp.clip(at, 0, total.shape[1] - quarter)
            slot = quarter * block + lax.broadcasted_iota(jnp.int32, (quarter, 1), 0)
            value = jnp.concatenate([total[tile, pl.ds(at, quarter), :] for tile in range(tiles)], axis=1)
            return jnp.where(slot < counts[owner], value, 0.0)[:, :size]

        for ref, side in ((keep_ref, core), (send_ref, 1 - core)):
            ref[:quarter] = rows(1, side)
            ref[quarter : 2 * quarter] = rows(1, side + 2)
            ref[2 * quarter : 3 * quarter] = rows(0, side) + rows(0, side + 2)
            ref[3 * quarter :] = rows(2, side)


def translate(owner_count, group_count, own, own_peer, near, near_peer, weights, picks, boxes):
    offsets, capacity, span = picks.shape
    size = weights.shape[1]
    width = weights.shape[2]
    quarter = own.shape[0] // 2
    need = capacity + 2 * (capacity // 3)
    tiles = padded(size) // LANES
    smem = pl.BlockSpec(memory_space=pltpu.SMEM)
    vmem = pl.BlockSpec(memory_space=pltpu.VMEM)
    return pl.pallas_call(
        functools.partial(
            translate_kernel,
            boxes=boxes,
            capacity=capacity,
            quarter=quarter,
            size=size,
            span=span,
            need=need,
        ),
        grid=(offsets,),
        in_specs=[
            smem,
            smem,
            vmem,
            vmem,
            vmem,
            vmem,
            pl.BlockSpec((1, size, width), lambda k: (k, 0, 0)),
            pl.BlockSpec((1, capacity, span), lambda k: (k, 0, 0)),
        ],
        out_specs=[vmem, vmem],
        out_shape=[jax.ShapeDtypeStruct((capacity, size), jnp.float32)] * 2,
        scratch_shapes=[
            pltpu.VMEM((tiles, 3 * capacity, LANES), jnp.float32),
            pltpu.VMEM((span, width), jnp.bfloat16),
            pltpu.VMEM((tiles, 3 * capacity, LANES), jnp.float32),
        ],
        name="translate",
    )(owner_count, group_count, own, own_peer, near, near_peer, weights, picks)


def body(density, operators, owner_count, group_count, target_slot, source_box):
    quarter = density.shape[0]
    parts = lax.axis_size("op")
    boxes = lax.axis_size("box")
    capacity = quarter * parts
    if parts != 4:
        raise ValueError("unsupported op axis")
    span = padded(capacity + 2 * (capacity // 3))
    device = lax.axis_index("op")

    earlier = to_box(density, 1)
    later = to_box(density, -1)
    across = flip(density, 2)
    weights = split_operators(operators)
    picks, side = selections(
        owner_count, group_count, target_slot, source_box, boxes, quarter, span
    )
    own = jnp.concatenate([density, across], axis=0)
    own_peer = flip(own, 1)
    near = jnp.concatenate([earlier, later], axis=0)
    near = jnp.concatenate([near, flip(near, 2)], axis=0)
    near_peer = flip(near, 1)
    send, keep = translate(
        owner_count, group_count, own, own_peer, near, near_peer, weights, picks, boxes
    )
    both = keep + flip(send, 1)
    low, high, down, up = (both[i * quarter : (i + 1) * quarter] for i in range(4))
    from_after = to_box(down, -1)
    from_before = to_box(up, 1)
    early = side[:, :1] > 0.5
    low = low + from_before + jnp.where(early, from_after, 0.0)
    high = high + jnp.where(early, 0.0, from_after)
    first = device < 2
    return jnp.where(first, low, high) + flip(jnp.where(first, high, low), 2)


def solution(mesh):
    placed = (
        P(("box", "op"), None),
        P("op", None, None),
        P(),
        P(),
        P("box", "op", None),
        P("box", "op", None),
    )
    return jax.shard_map(
        body, mesh=mesh, in_specs=placed, out_specs=P(("box", "op"), None), check_vma=False
    )
```

time: 128 us -> 75.6 us (0.59)
  Pallas kernels: 0 us -> 34.2 us
  blocking collectives: 26.6 us -> 0 us
  matrix products: 19.9 us -> 0 us
  local copies, waits for them, and re-layouts: 20.2 us -> 1.91 us
  waiting for transfers between devices: 31.2 us -> 18.4 us
  other arithmetic: 10.5 us -> 2.02 us
    pallas_call x0 -> x3, Pallas kernels: none -> 34.2 us  [the longest x1 18 us: translate(): pl.pallas_call(functools.partial(translate_kernel, boxes=boxes, capacity=...]
    dot_general x1 -> x0, matrix products: 19.9 us -> none  [body(): jnp.einsum('jkl,kil->ji', source_rows, operators, precision=lax.Precision...]
    gather x3 -> x0, local copies, waits for them, and re-layouts: 15 us -> none  [the longest x1 12.2 us: body(): source_rows = jnp.where(live_mask, window[source_ids], 0.0)]
    ppermute x6 -> x10, waiting for transfers between devices: 31.2 us -> 18.4 us  [the longest x6 11.2 us: flip(): return lax.ppermute(block, 'op', [(i, i ^ bit) for i in range(count)])]
    unnamed x1 -> x0, blocking collectives: 10.1 us -> none
    all_gather x1 -> x0, blocking collectives: 8.4 us -> none  [body(): owned_rows = lax.all_gather(density, 'op', axis=0, tiled=True)]
    all_to_all x1 -> x0, blocking collectives: 8.18 us -> none  [body(): lax.all_to_all(returned, 'op', split_axis=0, concat_axis=1, tiled=True)]
    select_n x5 -> x1, other arithmetic: 7.19 us -> 0.09 us  [body(): return jnp.where(first, low, high) + flip(jnp.where(first, high, low), 2)]
  transfers between devices with their start and end apart: 7 -> 10, of which waited for: 4 -> 6; matrix products, arithmetic and copies ran while one was open for 11% -> 2% of each run, Pallas kernels for 0% -> 22%
where the time goes in v1:
time: 75.6 us; the launch traced here: 74.7 us
  Pallas kernels  34.2 us (45%)
  waiting for transfers between devices  18.4 us (24%)
  starting transfers between devices  18.1 us (24%)
  other arithmetic  2.02 us (3%)
  local copies, waits for them, and re-layouts  1.91 us (3%)
    pallas_call x1, Pallas kernels, translate(): pl.pallas_call(functools.partial(translate_kernel, boxes=boxes, capacity=...  18 us
    ppermute x4, starting transfers between devices, to_box(): return lax.ppermute(block, 'box', shifted('box', step))  12.5 us
    pallas_call x1, Pallas kernels, split_operators(): pl.pallas_call(functools.partial(operator_kernel, size=size, whole=whole)...  12.1 us
    ppermute x6, waiting for transfers between devices, flip(): return lax.ppermute(block, 'op', [(i, i ^ bit) for i in range(count)])  11.2 us
    ppermute x4, waiting for transfers between devices, to_box(): return lax.ppermute(block, 'box', shifted('box', step))  7.19 us
    ppermute x6, starting transfers between devices, flip(): return lax.ppermute(block, 'op', [(i, i ^ bit) for i in range(count)])  5.61 us
    pallas_call x1, Pallas kernels, selections(): pl.pallas_call(functools.partial(select_kernel, boxes=boxes, capacity=cap...  4.11 us
    unnamed x13, local copies, waits for them, and re-layouts  1.87 us
  transfers between devices with their start and end apart: 10, of which 6 were waited for; matrix products, arithmetic and copies ran while one was open for 2% of the time, Pallas kernels for 22%

profile of v1, /device:TPU:0, one launch (start us, length us, event | category | flops | bytes accessed | tf_op | source)
XLA Modules:
  0.0 74.7 jit_solution(10780492119172891230)
XLA Ops:
  0.0 1.3 %collective-permute-start.3 = (f32[72,296]{1,0:T(8,128)}, f32[72,296]{1,0:T(8,128)S(1)}, u32[]{:S(2)}, u32[]{:S(2)}) collective-permute-start(f32[72,296]{1,0:T(8,128)} %param.6), channel_id=1, source_target_pairs={{4,0},{8,4},{12,8},{16,12},{20,16},{24,20},{28,24},{5,1},{9,5},{13... | collective-permute-start | bytes 255752 | tf_op jit(solution)/shard_map/ppermute | solution.py:28
  1.3 5.5 %collective-permute-start.2 = (f32[72,296]{1,0:T(8,128)}, f32[72,296]{1,0:T(8,128)S(1)}, u32[]{:S(2)}, u32[]{:S(2)}) collective-permute-start(f32[72,296]{1,0:T(8,128)} %param.6), channel_id=1, source_target_pairs={{0,4},{4,8},{8,12},{12,16},{16,20},{20,24},{24,28},{1,5},{5,9},{9,... | collective-permute-start | bytes 255752 | tf_op jit(solution)/shard_map/ppermute | solution.py:28
  6.8 2.1 %collective-permute-start = (f32[72,296]{1,0:T(8,128)}, f32[72,296]{1,0:T(8,128)S(1)}, u32[]{:S(2)}, u32[]{:S(2)}) collective-permute-start(f32[72,296]{1,0:T(8,128)} %param.6), channel_id=1, source_target_pairs={{0,2},{1,3},{2,0},{3,1},{4,6},{5,7},{6,4},{7,5},{8,10},{9,11},{10,... | collective-permute-start | bytes 255752 | tf_op jit(solution)/shard_map/ppermute | solution.py:24
  8.9 0.0 collective-permute-done.3
  8.9 1.9 %collective-permute-done.2 = f32[72,296]{1,0:T(8,128)S(1)} collective-permute-done((f32[72,296]{1,0:T(8,128)}, f32[72,296]{1,0:T(8,128)S(1)}, u32[]{:S(2)}, u32[]{:S(2)}) %collective-permute-start.2) | collective-permute-done | bytes 85280 | tf_op jit(solution)/shard_map/ppermute | solution.py:28
  10.8 1.6 %collective-permute-start.4 = (f32[144,296]{1,0:T(8,128)S(1)}, f32[144,296]{1,0:T(8,128)S(1)}, u32[]{:S(2)}, u32[]{:S(2)}) collective-permute-start(f32[144,296]{1,0:T(8,128)S(1)} %pad_maximum_fusion), channel_id=1, source_target_pairs={{0,2},{1,3},{2,0},{3,1},{4,6},{5,7},{6,4},{7,5},{8,10},{9,11},{10,... | collective-permute-start | bytes 511496 | tf_op jit(solution)/shard_map/ppermute | solution.py:24
  12.4 5.8 %collective-permute-done.4 = f32[144,296]{1,0:T(8,128)S(1)} collective-permute-done((f32[144,296]{1,0:T(8,128)S(1)}, f32[144,296]{1,0:T(8,128)S(1)}, u32[]{:S(2)}, u32[]{:S(2)}) %collective-permute-start.4) | collective-permute-done | bytes 170528 | tf_op jit(solution)/shard_map/ppermute | solution.py:24
  18.2 0.1 collective-permute-start.5
  18.3 1.0 %constant_dynamic-update-slice_fusion.1 = f32[144,296]{1,0:T(8,128)S(1)} fusion(f32[72,296]{1,0:T(8,128)} %param.6), kind=kLoop, calls=%fused_computation.9 | loop fusion | bytes 195840
  19.3 0.0 collective-permute-done
  19.3 0.0 copy-start.1
  19.4 0.5 collective-permute-start.1
  19.8 12.1 %split_operators.1.weight_ref = bf16[16,296,640]{2,1,0:T(8,128)(2,1)} custom-call(f32[16,296,296]{2,1,0:T(8,128)} %op_ref.1), custom_call_target="tpu_custom_call" | custom-call | bytes 11669504 | tf_op jit(solution)/shard_map/split_operators/pallas_call | solution.py:69
  31.9 4.1 %selections.1 = (bf16[16,288,512]{2,1,0:T(8,128)(2,1)}, f32[72,128]{1,0:T(8,128)}) custom-call(s32[8]{0:T(128)} %owner_ref.3, s32[8]{0:T(128)} %group_ref.3, s32[1,16,288]{2,1,0:T(8,128)} %target_ref.1, s32[1,16,288]{2,1,0:T(8,128)} %source_ref.1), custom_call_target="tpu_custom_call" | custom-call | bytes 4718592 | tf_op jit(solution)/shard_map/selections/pallas_call | solution.py:107
  36.0 0.0 collective-permute-done.1.own_peer_ref
  36.0 0.0 collective-permute-done.5.near_peer_ref
  36.1 0.0 copy-start.2
  36.1 0.7 copy-done.3
  36.7 0.2 copy-done.2
  36.9 18.0 %translate.1 = (f32[288,296]{1,0:T(8,128)}, f32[288,296]{1,0:T(8,128)}) custom-call(s32[8]{0:T(128)} %owner_ref.3, s32[8]{0:T(128)} %group_ref.3, f32[144,296]{1,0:T(8,128)} %copy-done.1, f32[144,296]{1,0:T(8,128)} %copy-done.3, f32[288,296]{1,0:T(8,128)} %copy-done, f32[288,296]{1,0:T(8,128)} %copy-done.2, bf16[16,296,640]{2,1,0:T(8,128)(2,1)} %split_operators.1.weight_ref, ...), custom_call_target="tpu_custom_call" | custom-call | tf_op jit(solution)/shard_map/translate/pallas_call | solution.py:238
  54.9 0.1 collective-permute-start.6
  55.0 1.9 %collective-permute-done.6 = f32[288,296]{1,0:T(8,128)S(1)} collective-permute-done((f32[288,296]{1,0:T(8,128)}, f32[288,296]{1,0:T(8,128)S(1)}, u32[]{:S(2)}, u32[]{:S(2)}) %collective-permute-start.6) | collective-permute-done | bytes 341024 | tf_op jit(solution)/shard_map/ppermute | solution.py:24
  56.9 1.1 %add.15 = f32[288,296]{1,0:T(8,128)S(1)} add(f32[288,296]{1,0:T(8,128)} %get-tuple-element.10, f32[288,296]{1,0:T(8,128)S(1)} %collective-permute-done.6) | non-fusion elementwise | flops 85248 | bytes 1022976 | tf_op jit(solution)/shard_map/add | solution.py:295
  58.0 4.3 %collective-permute-start.7 = (f32[72,296]{1,0:T(8,128)S(1)}, f32[72,296]{1,0:T(8,128)S(1)}, u32[]{:S(2)}, u32[]{:S(2)}) collective-permute-start(f32[72,296]{1,0:T(8,128)S(1)} %get-tuple-element.13), channel_id=1, source_target_pairs={{0,4},{4,8},{8,12},{12,16},{16,20},{20,24},{24,28},{1,5},{5,9},{9,... | collective-permute-start | bytes 255752 | tf_op jit(solution)/shard_map/ppermute | solution.py:28
  62.4 1.3 %collective-permute-start.8 = (f32[72,296]{1,0:T(8,128)S(1)}, f32[72,296]{1,0:T(8,128)S(1)}, u32[]{:S(2)}, u32[]{:S(2)}) collective-permute-start(f32[72,296]{1,0:T(8,128)S(1)} %get-tuple-element.14), channel_id=1, source_target_pairs={{4,0},{8,4},{12,8},{16,12},{20,16},{24,20},{28,24},{5,1},{9,5},{13... | collective-permute-start | bytes 255752 | tf_op jit(solution)/shard_map/ppermute | solution.py:28
  63.7 0.1 fusion.1
  63.8 1.2 %collective-permute-done.7 = f32[72,296]{1,0:T(8,128)S(1)} collective-permute-done((f32[72,296]{1,0:T(8,128)S(1)}, f32[72,296]{1,0:T(8,128)S(1)}, u32[]{:S(2)}, u32[]{:S(2)}) %collective-permute-start.7) | collective-permute-done | bytes 85280 | tf_op jit(solution)/shard_map/ppermute | solution.py:28
  64.9 4.1 %collective-permute-done.8 = f32[72,296]{1,0:T(8,128)S(1)} collective-permute-done((f32[72,296]{1,0:T(8,128)S(1)}, f32[72,296]{1,0:T(8,128)S(1)}, u32[]{:S(2)}, u32[]{:S(2)}) %collective-permute-start.8) | collective-permute-done | bytes 85280 | tf_op jit(solution)/shard_map/ppermute | solution.py:28
  69.1 0.1 broadcast_select_fusion
  69.2 1.4 %collective-permute-start.9 = (f32[72,296]{1,0:T(8,128)S(1)}, f32[72,296]{1,0:T(8,128)S(1)}, u32[]{:S(2)}, u32[]{:S(2)}) collective-permute-start(f32[72,296]{1,0:T(8,128)S(1)} %broadcast_select_fusion), channel_id=1, source_target_pairs={{0,2},{1,3},{2,0},{3,1},{4,6},{5,7},{6,4},{7,5},{8,10},{9,11},{10,... | collective-permute-start | bytes 255752 | tf_op jit(solution)/shard_map/ppermute | solution.py:24
  70.5 3.5 %collective-permute-done.9 = f32[72,296]{1,0:T(8,128)S(1)} collective-permute-done((f32[72,296]{1,0:T(8,128)S(1)}, f32[72,296]{1,0:T(8,128)S(1)}, u32[]{:S(2)}, u32[]{:S(2)}) %collective-permute-start.9) | collective-permute-done | bytes 85280 | tf_op jit(solution)/shard_map/ppermute | solution.py:24
  74.0 0.7 select_add_fusion
  (12 shorter events, 0.1 us)
Async XLA Ops:
  0.0 8.9 %collective-permute-start.3 = (f32[72,296]{1,0:T(8,128)}, f32[72,296]{1,0:T(8,128)S(1)}, u32[]{:S(2)}, u32[]{:S(2)}) collective-permute-start(f32[72,296]{1,0:T(8,128)} %param.6), channel_id=1, source_target_pairs={{4,0},{8,4},{12,8},{16,12},{20,16},{24,20},{28,24},{5,1},{9,5},{13... | collective-permute-start | bytes 255752 | tf_op jit(solution)/shard_map/ppermute | solution.py:28
  1.3 9.5 %collective-permute-start.2 = (f32[72,296]{1,0:T(8,128)}, f32[72,296]{1,0:T(8,128)S(1)}, u32[]{:S(2)}, u32[]{:S(2)}) collective-permute-start(f32[72,296]{1,0:T(8,128)} %param.6), channel_id=1, source_target_pairs={{0,4},{4,8},{8,12},{12,16},{16,20},{20,24},{24,28},{1,5},{5,9},{9,... | collective-permute-start | bytes 255752 | tf_op jit(solution)/shard_map/ppermute | solution.py:28
  6.8 12.5 %collective-permute-start = (f32[72,296]{1,0:T(8,128)}, f32[72,296]{1,0:T(8,128)S(1)}, u32[]{:S(2)}, u32[]{:S(2)}) collective-permute-start(f32[72,296]{1,0:T(8,128)} %param.6), channel_id=1, source_target_pairs={{0,2},{1,3},{2,0},{3,1},{4,6},{5,7},{6,4},{7,5},{8,10},{9,11},{10,... | collective-permute-start | bytes 255752 | tf_op jit(solution)/shard_map/ppermute | solution.py:24
  10.8 7.4 %collective-permute-start.4 = (f32[144,296]{1,0:T(8,128)S(1)}, f32[144,296]{1,0:T(8,128)S(1)}, u32[]{:S(2)}, u32[]{:S(2)}) collective-permute-start(f32[144,296]{1,0:T(8,128)S(1)} %pad_maximum_fusion), channel_id=1, source_target_pairs={{0,2},{1,3},{2,0},{3,1},{4,6},{5,7},{6,4},{7,5},{8,10},{9,11},{10,... | collective-permute-start | bytes 511496 | tf_op jit(solution)/shard_map/ppermute | solution.py:24
  18.2 13.7 %copy-start = (f32[288,296]{1,0:T(8,128)}, f32[288,296]{1,0:T(8,128)S(1)}, u32[]{:S(2)}) copy-start(f32[288,296]{1,0:T(8,128)S(1)} %constant_dynamic-update-slice_fusion.2.near_ref) | copy-start | bytes 1022980
  18.2 17.8 %collective-permute-start.5 = (f32[288,296]{1,0:T(8,128)S(1)}, f32[288,296]{1,0:T(8,128)S(1)}, u32[]{:S(2)}, u32[]{:S(2)}) collective-permute-start(f32[288,296]{1,0:T(8,128)S(1)} %constant_dynamic-update-slice_fusion.2.near_ref), channel_id=1, source_target_pairs={{0,1},{1,0},{2,3},{3,2},{4,5},{5,4},{6,7},{7,6},{8,9},{9,8},{10,11... | collective-permute-start | bytes 1022984 | tf_op jit(solution)/shard_map/ppermute | solution.py:24
  19.3 12.6 %copy-start.1 = (f32[144,296]{1,0:T(8,128)}, f32[144,296]{1,0:T(8,128)S(1)}, u32[]{:S(2)}) copy-start(f32[144,296]{1,0:T(8,128)S(1)} %constant_dynamic-update-slice_fusion.own_ref) | copy-start | bytes 511492
  19.4 16.7 %collective-permute-start.1 = (f32[144,296]{1,0:T(8,128)S(1)}, f32[144,296]{1,0:T(8,128)S(1)}, u32[]{:S(2)}, u32[]{:S(2)}) collective-permute-start(f32[144,296]{1,0:T(8,128)S(1)} %constant_dynamic-update-slice_fusion.own_ref), channel_id=1, source_target_pairs={{0,1},{1,0},{2,3},{3,2},{4,5},{5,4},{6,7},{7,6},{8,9},{9,8},{10,11... | collective-permute-start | bytes 511496 | tf_op jit(solution)/shard_map/ppermute | solution.py:24
  36.0 0.7 copy-start.3
  36.1 0.9 %copy-start.2 = (f32[288,296]{1,0:T(8,128)}, f32[288,296]{1,0:T(8,128)S(1)}, u32[]{:S(2)}) copy-start(f32[288,296]{1,0:T(8,128)S(1)} %collective-permute-done.5.near_peer_ref) | copy-start | bytes 1022980
  36.9 26.7 %copy-start.4 = (f32[72,128]{1,0:T(8,128)S(1)}, f32[72,128]{1,0:T(8,128)}, u32[]{:S(2)}) copy-start(f32[72,128]{1,0:T(8,128)} %get-tuple-element.12) | copy-start | bytes 110596
  54.9 2.0 %collective-permute-start.6 = (f32[288,296]{1,0:T(8,128)}, f32[288,296]{1,0:T(8,128)S(1)}, u32[]{:S(2)}, u32[]{:S(2)}) collective-permute-start(f32[288,296]{1,0:T(8,128)} %get-tuple-element.11), channel_id=1, source_target_pairs={{0,1},{1,0},{2,3},{3,2},{4,5},{5,4},{6,7},{7,6},{8,9},{9,8},{10,11... | collective-permute-start | bytes 1022984 | tf_op jit(solution)/shard_map/ppermute | solution.py:24
  58.0 6.9 %collective-permute-start.7 = (f32[72,296]{1,0:T(8,128)S(1)}, f32[72,296]{1,0:T(8,128)S(1)}, u32[]{:S(2)}, u32[]{:S(2)}) collective-permute-start(f32[72,296]{1,0:T(8,128)S(1)} %get-tuple-element.13), channel_id=1, source_target_pairs={{0,4},{4,8},{8,12},{12,16},{16,20},{20,24},{24,28},{1,5},{5,9},{9,... | collective-permute-start | bytes 255752 | tf_op jit(solution)/shard_map/ppermute | solution.py:28
  62.4 6.7 %collective-permute-start.8 = (f32[72,296]{1,0:T(8,128)S(1)}, f32[72,296]{1,0:T(8,128)S(1)}, u32[]{:S(2)}, u32[]{:S(2)}) collective-permute-start(f32[72,296]{1,0:T(8,128)S(1)} %get-tuple-element.14), channel_id=1, source_target_pairs={{4,0},{8,4},{12,8},{16,12},{20,16},{24,20},{28,24},{5,1},{9,5},{13... | collective-permute-start | bytes 255752 | tf_op jit(solution)/shard_map/ppermute | solution.py:28
  69.2 4.8 %collective-permute-start.9 = (f32[72,296]{1,0:T(8,128)S(1)}, f32[72,296]{1,0:T(8,128)S(1)}, u32[]{:S(2)}, u32[]{:S(2)}) collective-permute-start(f32[72,296]{1,0:T(8,128)S(1)} %broadcast_select_fusion), channel_id=1, source_target_pairs={{0,2},{1,3},{2,0},{3,1},{4,6},{5,7},{6,4},{7,5},{8,10},{9,11},{10,... | collective-permute-start | bytes 255752 | tf_op jit(solution)/shard_map/ppermute | solution.py:24

commit v2 on v1

v2 whole, which is shorter than its diff:
```python
import functools
import math

import jax
import jax.numpy as jnp
from jax import lax
from jax.experimental import pallas as pl
from jax.experimental.pallas import tpu as pltpu
from jax.sharding import PartitionSpec as P

LANES = 128
GRANT = 20 << 20
BATCH = 2


def padded(size, to=LANES):
    return -(-size // to) * to


def shifted(pairs_axis, step):
    count = lax.axis_size(pairs_axis)
    return [(i, i + step) for i in range(count) if 0 <= i + step < count]


def flip(block, bit):
    count = lax.axis_size("op")
    return lax.ppermute(block, "op", [(i, i ^ bit) for i in range(count)])


def to_box(block, step):
    return lax.ppermute(block, "box", shifted("box", step))


def prefix(count_ref, upto):
    return lax.fori_loop(0, upto, lambda i, total: total + count_ref[i], 0)


def places(owner_ref, group_ref, box, boxes, capacity):
    before = jnp.maximum(box - 1, 0)
    after = jnp.minimum(box + 1, boxes - 1)
    own_start = prefix(owner_ref, box)
    own_count = owner_ref[box]
    prev_count = jnp.where(box > 0, owner_ref[before], 0)
    prev_start = own_start - jnp.where(box > 0, prev_count, capacity)
    next_start = own_start + own_count
    next_count = jnp.where(box < boxes - 1, owner_ref[after], 0)
    return (
        (prev_start, own_start, next_start),
        (prev_count, own_count, next_count),
        prefix(group_ref, box),
    )


def operator_kernel(op_ref, main_ref, rest_ref, *, size, whole, room):
    tail = size - whole

    def split(k, carry):
        block = op_ref[k]
        high = block.astype(jnp.bfloat16)
        wide = high.astype(jnp.float32)
        low = block - wide
        space = jnp.zeros((size, LANES - tail), jnp.float32)
        high_tail = jnp.concatenate([wide[:, whole:], space], axis=1)
        low_tail = jnp.concatenate([low[:, whole:], space], axis=1)
        ends = high_tail + pltpu.roll(high_tail, tail, 1) + pltpu.roll(low_tail, 2 * tail, 1)
        low = low[:, :whole].astype(jnp.bfloat16)
        ends = ends.astype(jnp.bfloat16)
        main_ref[k, :, :whole] = high[:whole, :whole]
        main_ref[k, :, whole : 2 * whole] = low[:whole]
        main_ref[k, :, 2 * whole :] = ends[:whole]
        blank = jnp.zeros((room - tail, whole), jnp.bfloat16)
        first = jnp.concatenate([high[whole:, :whole], blank], axis=0)
        rest_ref[k, :room, :whole] = first
        rest_ref[k, :room, whole : 2 * whole] = first
        rest_ref[k, :room, 2 * whole :] = jnp.concatenate([ends[whole:], blank[:, :LANES]], axis=0)
        rest_ref[k, room:, :whole] = jnp.concatenate([low[whole:], blank], axis=0)
        rest_ref[k, room:, whole:] = jnp.zeros((room, whole + LANES), jnp.bfloat16)
        return carry

    lax.fori_loop(0, op_ref.shape[0], split, 0)


def split_operators(operators):
    count, size, _ = operators.shape
    whole = size // LANES * LANES
    room = padded(size - whole, 16)
    width = 2 * whole + LANES
    vmem = pl.BlockSpec(memory_space=pltpu.VMEM)
    return pl.pallas_call(
        functools.partial(operator_kernel, size=size, whole=whole, room=room),
        in_specs=[vmem],
        out_specs=[vmem, vmem],
        out_shape=[
            jax.ShapeDtypeStruct((count, whole, width), jnp.bfloat16),
            jax.ShapeDtypeStruct((count, 2 * room, width), jnp.bfloat16),
        ],
        compiler_params=pltpu.CompilerParams(vmem_limit_bytes=GRANT),
        cost_estimate=pl.CostEstimate(
            flops=0, transcendentals=0, bytes_accessed=count * size * (4 * size + 2 * width)
        ),
        name="split_operators",
    )(operators)


def select_kernel(owner_ref, group_ref, target_ref, source_ref, out_ref, side_ref, *, boxes, capacity, quarter, span):
    box = lax.axis_index("box")
    core = lax.axis_index("op") % 2
    starts, _, group_start = places(owner_ref, group_ref, box, boxes, capacity)
    first = group_start - capacity // 3
    alive = target_ref[0] < capacity
    found = jnp.where(alive, source_ref[0] - first, -1)
    offsets = found.shape[0]
    found = jnp.concatenate(
        [found, jnp.full((offsets, padded(capacity) - capacity), -1, jnp.int32)], axis=1
    )
    columns = found.T
    row = lax.broadcasted_iota(jnp.int32, (capacity, span), 1)
    for k in range(offsets):
        hit = columns[:capacity, k : k + 1] == row
        out_ref[k] = jnp.where(hit, 1.0, 0.0).astype(jnp.bfloat16)
    tail = group_start + group_ref[box] - starts[1]
    slot = quarter * core + lax.broadcasted_iota(jnp.int32, side_ref.shape, 0)
    side_ref[...] = jnp.where(slot >= tail, 1.0, 0.0)


def selections(owner_count, group_count, target_slot, source_box, boxes, quarter, span):
    _, offsets, capacity = target_slot.shape
    smem = pl.BlockSpec(memory_space=pltpu.SMEM)
    vmem = pl.BlockSpec(memory_space=pltpu.VMEM)
    return pl.pallas_call(
        functools.partial(
            select_kernel, boxes=boxes, capacity=capacity, quarter=quarter, span=span
        ),
        in_specs=[smem, smem, vmem, vmem],
        out_specs=[vmem, vmem],
        out_shape=[
            jax.ShapeDtypeStruct((offsets, capacity, span), jnp.bfloat16),
            jax.ShapeDtypeStruct((quarter, LANES), jnp.float32),
        ],
        compiler_params=pltpu.CompilerParams(vmem_limit_bytes=GRANT),
        cost_estimate=pl.CostEstimate(
            flops=0, transcendentals=0, bytes_accessed=2 * offsets * capacity * span
        ),
        name="selections",
    )(owner_count, group_count, target_slot, source_box)


def translate_kernel(
    owner_ref,
    group_ref,
    own_ref,
    own_peer_ref,
    near_ref,
    near_peer_ref,
    weight_ref,
    rest_ref,
    pick_ref,
    send_ref,
    keep_ref,
    window,
    packed,
    total,
    ends,
    *,
    boxes,
    capacity,
    quarter,
    size,
    span,
    need,
    batch,
):
    box = lax.axis_index("box")
    device = lax.axis_index("op")
    core = device % 2
    whole = size // LANES * LANES
    tail = size - whole
    third = capacity // 3
    tiles = padded(size) // LANES
    room = rest_ref.shape[1] // 2
    starts, counts, group_start = places(owner_ref, group_ref, box, boxes, capacity)

    def columns(tile):
        return slice(tile * LANES, min((tile + 1) * LANES, size))

    margin = 2 * third
    for tile in range(tiles):
        window[tile, margin + need : margin + span, :] = jnp.zeros((span - need, LANES), jnp.float32)
    for owner in range(3):
        for part in range(4):
            at = margin + starts[owner] + quarter * part - (group_start - third)
            at = jnp.clip(at, 0, window.shape[1] - quarter)
            mask = device ^ part
            line = pl.multiple_of(
                jnp.where(mask >= 2, quarter * (1 if owner == 1 else 2), 0)
                + (quarter if owner == 2 else 0),
                8,
            )
            mine, peers = (own_ref, own_peer_ref) if owner == 1 else (near_ref, near_peer_ref)

            def put(source):
                for tile in range(tiles):
                    lanes = columns(tile)
                    window[tile, pl.ds(at, quarter), : lanes.stop - lanes.start] = source[
                        pl.ds(line, quarter), lanes
                    ]

            pl.when(mask % 2 == 0)(functools.partial(put, mine))
            pl.when(mask % 2 == 1)(functools.partial(put, peers))
    for tile in range(tiles):
        value = window[tile, margin : margin + span, :]
        row = lax.broadcasted_iota(jnp.int32, value.shape, 0)
        lane = lax.broadcasted_iota(jnp.int32, value.shape, 1)
        fine = row < need
        if tile == tiles - 1:
            fine = fine & (lane < tail)
        value = jnp.where(fine, value, 0.0)
        high = value.astype(jnp.bfloat16)
        low = value - high.astype(jnp.float32)
        if tile < tiles - 1:
            packed[:, tile * LANES : (tile + 1) * LANES] = high
            packed[:, whole + tile * LANES : whole + (tile + 1) * LANES] = low.astype(jnp.bfloat16)
        else:
            high = high.astype(jnp.float32)
            rest = high + pltpu.roll(low, tail, 1) + pltpu.roll(high, 2 * tail, 1)
            packed[:, 2 * whole :] = rest.astype(jnp.bfloat16)
    total[...] = jnp.zeros(total.shape, jnp.float32)
    ends[...] = jnp.zeros(ends.shape, jnp.float32)

    def product(left, right):
        return lax.dot_general(
            jnp.concatenate(left, axis=1),
            jnp.concatenate(right, axis=1),
            (((1,), (1,)), ((), ())),
            preferred_element_type=jnp.float32,
        )

    def offsets(index, carry):
        base = index * batch
        picks = pick_ref[pl.ds(base, batch)].reshape(batch * capacity, span)
        picked = jnp.dot(picks, packed[...], preferred_element_type=jnp.float32).astype(jnp.bfloat16)
        left, right, left_ends, right_ends = [], [], [], []
        for i in range(batch):
            rows = picked[i * capacity : (i + 1) * capacity]
            weight = weight_ref[base + i]
            left += [rows[:, : 2 * whole], rows[:, :whole]]
            right += [weight[:, :whole], weight[:, : 2 * whole]]
            left_ends += [rows[:, : 2 * whole]]
            right_ends += [rest_ref[base + i, :, : 2 * whole]]
        for i in range(batch):
            last = picked[i * capacity : (i + 1) * capacity, 2 * whole :]
            left += [last]
            right += [weight_ref[base + i, :, 2 * whole :]]
            left_ends += [last]
            right_ends += [rest_ref[base + i, :, 2 * whole :]]
        part = product(left, right)
        for tile in range(tiles - 1):
            total[tile, capacity : 2 * capacity, :] += part[:, tile * LANES : (tile + 1) * LANES]
        ends[:, : 2 * room] += product(left_ends, right_ends)
        return carry

    lax.fori_loop(0, pick_ref.shape[0] // batch, offsets, 0)
    both = ends[...]
    total[tiles - 1, capacity : 2 * capacity, :] = both + pltpu.roll(both, LANES - room, 1)

    def rows(owner, block):
        at = capacity + starts[owner] - group_start + quarter * block
        at = jnp.clip(at, 0, total.shape[1] - quarter)
        slot = quarter * block + lax.broadcasted_iota(jnp.int32, (quarter, 1), 0)
        value = jnp.concatenate([total[tile, pl.ds(at, quarter), :] for tile in range(tiles)], axis=1)
        return jnp.where(slot < counts[owner], value, 0.0)[:, :size]

    for ref, side in ((keep_ref, core), (send_ref, 1 - core)):
        ref[:quarter] = rows(1, side)
        ref[quarter : 2 * quarter] = rows(1, side + 2)
        ref[2 * quarter : 3 * quarter] = rows(0, side) + rows(0, side + 2)
        ref[3 * quarter :] = rows(2, side)


def translate(owner_count, group_count, own, own_peer, near, near_peer, weights, rests, picks, boxes):
    offsets, capacity, span = picks.shape
    width = weights.shape[2]
    size = own.shape[1]
    quarter = own.shape[0] // 2
    need = capacity + 2 * (capacity // 3)
    tiles = padded(size) // LANES
    smem = pl.BlockSpec(memory_space=pltpu.SMEM)
    vmem = pl.BlockSpec(memory_space=pltpu.VMEM)
    return pl.pallas_call(
        functools.partial(
            translate_kernel,
            boxes=boxes,
            capacity=capacity,
            quarter=quarter,
            size=size,
            span=span,
            need=need,
            batch=math.gcd(offsets, BATCH),
        ),
        in_specs=[smem, smem] + [vmem] * 7,
        out_specs=[vmem, vmem],
        out_shape=[jax.ShapeDtypeStruct((capacity, size), jnp.float32)] * 2,
        scratch_shapes=[
            pltpu.VMEM((tiles, 3 * capacity, LANES), jnp.float32),
            pltpu.VMEM((span, width), jnp.bfloat16),
            pltpu.VMEM((tiles, 3 * capacity, LANES), jnp.float32),
            pltpu.VMEM((capacity, LANES), jnp.float32),
        ],
        compiler_params=pltpu.CompilerParams(vmem_limit_bytes=GRANT),
        name="translate",
    )(owner_count, group_count, own, own_peer, near, near_peer, weights, rests, picks)


def body(density, operators, owner_count, group_count, target_slot, source_box):
    quarter = density.shape[0]
    parts = lax.axis_size("op")
    boxes = lax.axis_size("box")
    capacity = quarter * parts
    if parts != 4:
        raise ValueError("unsupported op axis")
    span = padded(capacity + 2 * (capacity // 3))
    device = lax.axis_index("op")

    earlier = to_box(density, 1)
    later = to_box(density, -1)
    across = flip(density, 2)
    picks, side = selections(
        owner_count, group_count, target_slot, source_box, boxes, quarter, span
    )
    near = jnp.concatenate([earlier, later], axis=0)
    near, picks = lax.optimization_barrier((near, picks))
    near_across = flip(near, 2)
    own = jnp.concatenate([density, across], axis=0)
    own_peer = flip(own, 1)
    weights, rests = split_operators(operators)
    near_across, weights, rests = lax.optimization_barrier((near_across, weights, rests))
    near = jnp.concatenate([near, near_across], axis=0)
    near_peer = flip(near, 1)
    send, keep = translate(
        owner_count, group_count, own, own_peer, near, near_peer, weights, rests, picks, boxes
    )
    both = keep + flip(send, 1)
    low, high, down, up = (both[i * quarter : (i + 1) * quarter] for i in range(4))
    from_after = to_box(down, -1)
    from_before = to_box(up, 1)
    early = side[:, :1] > 0.5
    low = low + from_before + jnp.where(early, from_after, 0.0)
    high = high + jnp.where(early, 0.0, from_after)
    first = device < 2
    return jnp.where(first, low, high) + flip(jnp.where(first, high, low), 2)


def solution(mesh):
    placed = (
        P(("box", "op"), None),
        P("op", None, None),
        P(),
        P(),
        P("box", "op", None),
        P("box", "op", None),
    )
    return jax.shard_map(
        body, mesh=mesh, in_specs=placed, out_specs=P(("box", "op"), None), check_vma=False
    )
```

time: 75.6 us -> 51.5 us (0.68)
  Pallas kernels: 34.2 us -> 14 us
  waiting for transfers between devices: 18.4 us -> 13.3 us
  local copies, waits for them, and re-layouts: 1.91 us -> 5.92 us
  starting transfers between devices: 18.1 us -> 16.7 us
  other arithmetic: 2.02 us -> 1.01 us
    pallas_call x1, Pallas kernels: 12.1 us -> 2.35 us  [split_operators(): pl.pallas_call(functools.partial(operator_kernel, size=size, whole=whole,...]
    pallas_call x1, Pallas kernels: 18 us -> 9.99 us  [translate(): pl.pallas_call(functools.partial(translate_kernel, boxes=boxes, capacity=...]
    unnamed x13 -> x18, local copies, waits for them, and re-layouts: 1.87 us -> 5.88 us
    ppermute x6, waiting for transfers between devices: 11.2 us -> 8 us  [flip(): return lax.ppermute(block, 'op', [(i, i ^ bit) for i in range(count)])]
    pallas_call x1, Pallas kernels: 4.11 us -> 1.67 us  [selections(): pl.pallas_call(functools.partial(select_kernel, boxes=boxes, capacity=cap...]
    ppermute x4, waiting for transfers between devices: 7.19 us -> 5.31 us  [to_box(): return lax.ppermute(block, 'box', shifted('box', step))]
    ppermute x6, starting transfers between devices: 5.61 us -> 4.02 us  [flip(): return lax.ppermute(block, 'op', [(i, i ^ bit) for i in range(count)])]
    add x1, other arithmetic: 1.06 us -> 0.05 us  [body(): both = keep + flip(send, 1)]
  transfers between devices with their start and end apart: 10 -> 10, of which waited for: 6 -> 7; matrix products, arithmetic and copies ran while one was open for 2% -> 0% of each run, Pallas kernels for 22% -> 8%
where the time goes in v2:
time: 51.5 us; the launch traced here: 51.1 us
  starting transfers between devices  16.7 us (32%)
  Pallas kernels  14 us (27%)
  waiting for transfers between devices  13.3 us (26%)
  local copies, waits for them, and re-layouts  5.92 us (11%)
  other arithmetic  1.01 us (2%)
    ppermute x4, starting transfers between devices, to_box(): return lax.ppermute(block, 'box', shifted('box', step))  12.7 us
    pallas_call x1, Pallas kernels, translate(): pl.pallas_call(functools.partial(translate_kernel, boxes=boxes, capacity=...  9.99 us
    ppermute x6, waiting for transfers between devices, flip(): return lax.ppermute(block, 'op', [(i, i ^ bit) for i in range(count)])  8 us
    unnamed x18, local copies, waits for them, and re-layouts  5.88 us
    ppermute x4, waiting for transfers between devices, to_box(): return lax.ppermute(block, 'box', shifted('box', step))  5.31 us
    ppermute x6, starting transfers between devices, flip(): return lax.ppermute(block, 'op', [(i, i ^ bit) for i in range(count)])  4.02 us
    pallas_call x1, Pallas kernels, split_operators(): pl.pallas_call(functools.partial(operator_kernel, size=size, whole=whole,...  2.35 us
    pallas_call x1, Pallas kernels, selections(): pl.pallas_call(functools.partial(select_kernel, boxes=boxes, capacity=cap...  1.67 us
  transfers between devices with their start and end apart: 10, of which 7 were waited for; matrix products, arithmetic and copies ran while one was open for 0% of the time, Pallas kernels for 8%

profile of v2, /device:TPU:0, one launch (start us, length us, event | category | flops | bytes accessed | tf_op | source)
XLA Modules:
  0.0 51.1 jit_solution(9392696498705560636)
XLA Ops:
  0.0 1.3 %collective-permute-start.3 = (f32[72,296]{1,0:T(8,128)}, f32[72,296]{1,0:T(8,128)S(1)}, u32[]{:S(2)}, u32[]{:S(2)}) collective-permute-start(f32[72,296]{1,0:T(8,128)} %param.6), channel_id=1, source_target_pairs={{4,0},{8,4},{12,8},{16,12},{20,16},{24,20},{28,24},{5,1},{9,5},{13... | collective-permute-start | bytes 255752 | tf_op jit(solution)/shard_map/ppermute | solution.py:31
  1.3 5.5 %collective-permute-start.2 = (f32[72,296]{1,0:T(8,128)}, f32[72,296]{1,0:T(8,128)S(1)}, u32[]{:S(2)}, u32[]{:S(2)}) collective-permute-start(f32[72,296]{1,0:T(8,128)} %param.6), channel_id=1, source_target_pairs={{0,4},{4,8},{8,12},{12,16},{16,20},{20,24},{24,28},{1,5},{5,9},{9,... | collective-permute-start | bytes 255752 | tf_op jit(solution)/shard_map/ppermute | solution.py:31
  6.8 0.7 %copy-done.1 = s32[1,16,288]{2,1,0:T(8,128)S(1)} copy-done((s32[1,16,288]{2,1,0:T(8,128)S(1)}, s32[1,16,288]{2,1,0:T(8,128)}, u32[]{:S(2)}) %copy-start.1) | copy-done | bytes 18456
  7.6 0.7 %copy-done.2 = s32[1,16,288]{2,1,0:T(8,128)S(1)} copy-done((s32[1,16,288]{2,1,0:T(8,128)S(1)}, s32[1,16,288]{2,1,0:T(8,128)}, u32[]{:S(2)}) %copy-start.2) | copy-done | bytes 18456
  8.3 0.7 %copy-done.3 = s32[8]{0:T(128)S(1)} copy-done((s32[8]{0:T(128)S(1)}, s32[8]{0:T(128)}, u32[]{:S(2)}) %copy-start.3) | copy-done | bytes 56
  9.0 0.7 %copy-done.5 = s32[8]{0:T(128)S(1)} copy-done((s32[8]{0:T(128)S(1)}, s32[8]{0:T(128)}, u32[]{:S(2)}) %copy-start.5) | copy-done | bytes 56
  9.6 1.7 %selections.1 = (bf16[16,288,512]{2,1,0:T(8,128)(2,1)S(1)}, f32[72,128]{1,0:T(8,128)S(1)}) custom-call(s32[8]{0:T(128)S(1)} %copy-done.3, s32[8]{0:T(128)S(1)} %copy-done.5, s32[1,16,288]{2,1,0:T(8,128)S(1)} %copy-done.1, s32[1,16,288]{2,1,0:T(8,128)S(1)} %copy-done.2), custom_call_target="tpu_custom_call" | custom-call | bytes 4718592 | tf_op jit(solution)/shard_map/selections/pallas_call | solution.py:130
  11.3 0.0 collective-permute-done.3
  11.3 0.0 collective-permute-done.2
  11.4 2.1 %collective-permute-start.4 = (f32[144,296]{1,0:T(8,128)S(1)}, f32[144,296]{1,0:T(8,128)S(1)}, u32[]{:S(2)}, u32[]{:S(2)}) collective-permute-start(f32[144,296]{1,0:T(8,128)S(1)} %pad_maximum_fusion), channel_id=1, source_target_pairs={{0,2},{1,3},{2,0},{3,1},{4,6},{5,7},{6,4},{7,5},{8,10},{9,11},{10,... | collective-permute-start | bytes 511496 | tf_op jit(solution)/shard_map/ppermute | solution.py:27
  13.4 0.1 collective-permute-start
  13.5 3.1 %copy-done = f32[16,296,296]{2,1,0:T(8,128)S(1)} copy-done((f32[16,296,296]{2,1,0:T(8,128)S(1)}, f32[16,296,296]{2,1,0:T(8,128)}, u32[]{:S(2)}) %copy-start) | copy-done | bytes 5607448
  16.5 2.4 %split_operators.1 = (bf16[16,256,640]{2,1,0:T(8,128)(2,1)S(1)}, bf16[16,96,640]{2,1,0:T(8,128)(2,1)S(1)}) custom-call(f32[16,296,296]{2,1,0:T(8,128)S(1)} %copy-done), custom_call_target="tpu_custom_call" | custom-call | bytes 11669504 | tf_op jit(solution)/shard_map/split_operators/pallas_call | solution.py:89
  18.9 0.6 %collective-permute-done.4 = f32[144,296]{1,0:T(8,128)S(1)} collective-permute-done((f32[144,296]{1,0:T(8,128)S(1)}, f32[144,296]{1,0:T(8,128)S(1)}, u32[]{:S(2)}, u32[]{:S(2)}) %collective-permute-start.4) | collective-permute-done | bytes 170528 | tf_op jit(solution)/shard_map/ppermute | solution.py:27
  19.5 0.1 collective-permute-start.5
  19.6 1.1 %collective-permute-done = f32[72,296]{1,0:T(8,128)S(1)} collective-permute-done((f32[72,296]{1,0:T(8,128)}, f32[72,296]{1,0:T(8,128)S(1)}, u32[]{:S(2)}, u32[]{:S(2)}) %collective-permute-start) | collective-permute-done | bytes 85280 | tf_op jit(solution)/shard_map/ppermute | solution.py:27
  20.7 0.1 collective-permute-start.1
  20.8 1.5 %collective-permute-done.1.own_peer_ref = f32[144,296]{1,0:T(8,128)S(1)} collective-permute-done((f32[144,296]{1,0:T(8,128)S(1)}, f32[144,296]{1,0:T(8,128)S(1)}, u32[]{:S(2)}, u32[]{:S(2)}) %collective-permute-start.1) | collective-permute-done | bytes 170528 | tf_op jit(solution)/shard_map/ppermute | solution.py:27
  22.2 0.0 collective-permute-done.5.near_peer_ref
  22.2 0.0 copy-done.6
  22.2 10.0 %translate.1 = (f32[288,296]{1,0:T(8,128)S(1)}, f32[288,296]{1,0:T(8,128)S(1)}) custom-call(s32[8]{0:T(128)S(1)} %copy-done.4, s32[8]{0:T(128)S(1)} %copy-done.6, f32[144,296]{1,0:T(8,128)S(1)} %constant_dynamic-update-slice_fusion.own_ref, f32[144,296]{1,0:T(8,128)S(1)} %collective-permute-done.1.own_peer_ref, ...), custom_call_target="tpu_custom_call" | custom-call | tf_op jit(solution)/shard_map/translate/pallas_call | solution.py:289
  32.2 0.2 collective-permute-start.6
  32.4 1.7 %collective-permute-done.6 = f32[288,296]{1,0:T(8,128)S(1)} collective-permute-done((f32[288,296]{1,0:T(8,128)S(1)}, f32[288,296]{1,0:T(8,128)S(1)}, u32[]{:S(2)}, u32[]{:S(2)}) %collective-permute-start.6) | collective-permute-done | bytes 341024 | tf_op jit(solution)/shard_map/ppermute | solution.py:27
  34.2 4.6 %collective-permute-start.7 = (f32[72,296]{1,0:T(8,128)S(1)}, f32[72,296]{1,0:T(8,128)S(1)}, u32[]{:S(2)}, u32[]{:S(2)}) collective-permute-start(f32[72,296]{1,0:T(8,128)S(1)} %get-tuple-element.27), channel_id=1, source_target_pairs={{0,4},{4,8},{8,12},{12,16},{16,20},{20,24},{24,28},{1,5},{5,9},{9,... | collective-permute-start | bytes 255752 | tf_op jit(solution)/shard_map/ppermute | solution.py:31
  38.7 1.3 %collective-permute-start.8 = (f32[72,296]{1,0:T(8,128)S(1)}, f32[72,296]{1,0:T(8,128)S(1)}, u32[]{:S(2)}, u32[]{:S(2)}) collective-permute-start(f32[72,296]{1,0:T(8,128)S(1)} %get-tuple-element.28), channel_id=1, source_target_pairs={{4,0},{8,4},{12,8},{16,12},{20,16},{24,20},{28,24},{5,1},{9,5},{13... | collective-permute-start | bytes 255752 | tf_op jit(solution)/shard_map/ppermute | solution.py:31
  40.0 0.1 fusion.1
  40.2 1.2 %collective-permute-done.7 = f32[72,296]{1,0:T(8,128)S(1)} collective-permute-done((f32[72,296]{1,0:T(8,128)S(1)}, f32[72,296]{1,0:T(8,128)S(1)}, u32[]{:S(2)}, u32[]{:S(2)}) %collective-permute-start.7) | collective-permute-done | bytes 85280 | tf_op jit(solution)/shard_map/ppermute | solution.py:31
  41.3 4.1 %collective-permute-done.8 = f32[72,296]{1,0:T(8,128)S(1)} collective-permute-done((f32[72,296]{1,0:T(8,128)S(1)}, f32[72,296]{1,0:T(8,128)S(1)}, u32[]{:S(2)}, u32[]{:S(2)}) %collective-permute-start.8) | collective-permute-done | bytes 85280 | tf_op jit(solution)/shard_map/ppermute | solution.py:31
  45.5 0.1 broadcast_select_fusion
  45.6 1.6 %collective-permute-start.9 = (f32[72,296]{1,0:T(8,128)S(1)}, f32[72,296]{1,0:T(8,128)S(1)}, u32[]{:S(2)}, u32[]{:S(2)}) collective-permute-start(f32[72,296]{1,0:T(8,128)S(1)} %broadcast_select_fusion), channel_id=1, source_target_pairs={{0,2},{1,3},{2,0},{3,1},{4,6},{5,7},{6,4},{7,5},{8,10},{9,11},{10,... | collective-permute-start | bytes 255752 | tf_op jit(solution)/shard_map/ppermute | solution.py:27
  47.1 3.3 %collective-permute-done.9 = f32[72,296]{1,0:T(8,128)S(1)} collective-permute-done((f32[72,296]{1,0:T(8,128)S(1)}, f32[72,296]{1,0:T(8,128)S(1)}, u32[]{:S(2)}, u32[]{:S(2)}) %collective-permute-start.9) | collective-permute-done | bytes 85280 | tf_op jit(solution)/shard_map/ppermute | solution.py:27
  50.4 0.7 %select_add_fusion = f32[72,296]{1,0:T(8,128)} fusion(f32[72,296]{1,0:T(8,128)S(1)} %collective-permute-done.9, pred[]{:T(512)S(6)} %lt.3, f32[72,296]{1,0:T(8,128)S(1)} %collective-permute-done.8, pred[72]{0:T(512)(128)(4,1)S(1)} %fusion.1, f32[288,296]{1,0:T(8,128)S(1)} %add.15, f32[72,296]{1,0:T(8,128)S(1)} %collective-permute-done.7), kind=kLoop, calls=%fused_computation.4 | loop fusion | flops 149184 | bytes 511561 | tf_op jit(solution)/shard_map/add | solution.py:350
  (17 shorter events, 0.1 us)
Async XLA Ops:
  0.0 11.3 %collective-permute-start.3 = (f32[72,296]{1,0:T(8,128)}, f32[72,296]{1,0:T(8,128)S(1)}, u32[]{:S(2)}, u32[]{:S(2)}) collective-permute-start(f32[72,296]{1,0:T(8,128)} %param.6), channel_id=1, source_target_pairs={{4,0},{8,4},{12,8},{16,12},{20,16},{24,20},{28,24},{5,1},{9,5},{13... | collective-permute-start | bytes 255752 | tf_op jit(solution)/shard_map/ppermute | solution.py:31
  1.3 10.0 %collective-permute-start.2 = (f32[72,296]{1,0:T(8,128)}, f32[72,296]{1,0:T(8,128)S(1)}, u32[]{:S(2)}, u32[]{:S(2)}) collective-permute-start(f32[72,296]{1,0:T(8,128)} %param.6), channel_id=1, source_target_pairs={{0,4},{4,8},{8,12},{12,16},{16,20},{20,24},{24,28},{1,5},{5,9},{9,... | collective-permute-start | bytes 255752 | tf_op jit(solution)/shard_map/ppermute | solution.py:31
  6.8 0.7 %copy-start.1 = (s32[1,16,288]{2,1,0:T(8,128)S(1)}, s32[1,16,288]{2,1,0:T(8,128)}, u32[]{:S(2)}) copy-start(s32[1,16,288]{2,1,0:T(8,128)} %target_ref.1) | copy-start | bytes 55300
  7.6 0.7 %copy-start.2 = (s32[1,16,288]{2,1,0:T(8,128)S(1)}, s32[1,16,288]{2,1,0:T(8,128)}, u32[]{:S(2)}) copy-start(s32[1,16,288]{2,1,0:T(8,128)} %source_ref.1) | copy-start | bytes 55300
  8.3 0.7 %copy-start.3 = (s32[8]{0:T(128)S(1)}, s32[8]{0:T(128)}, u32[]{:S(2)}) copy-start(s32[8]{0:T(128)} %owner_ref.3) | copy-start | bytes 100
  9.0 0.7 %copy-start.5 = (s32[8]{0:T(128)S(1)}, s32[8]{0:T(128)}, u32[]{:S(2)}) copy-start(s32[8]{0:T(128)} %group_ref.3) | copy-start | bytes 100
  9.6 10.0 %copy-start.7 = (f32[72,296]{1,0:T(8,128)S(1)}, f32[72,296]{1,0:T(8,128)}, u32[]{:S(2)}) copy-start(f32[72,296]{1,0:T(8,128)} %param.6) | copy-start | bytes 255748
  9.6 12.6 %copy-start.4 = (s32[8]{0:T(128)S(1)}, s32[8]{0:T(128)}, u32[]{:S(2)}) copy-start(s32[8]{0:T(128)} %owner_ref.3) | copy-start | bytes 100
  9.6 12.6 %copy-start.6 = (s32[8]{0:T(128)S(1)}, s32[8]{0:T(128)}, u32[]{:S(2)}) copy-start(s32[8]{0:T(128)} %group_ref.3) | copy-start | bytes 100
  11.4 8.1 %collective-permute-start.4 = (f32[144,296]{1,0:T(8,128)S(1)}, f32[144,296]{1,0:T(8,128)S(1)}, u32[]{:S(2)}, u32[]{:S(2)}) collective-permute-start(f32[144,296]{1,0:T(8,128)S(1)} %pad_maximum_fusion), channel_id=1, source_target_pairs={{0,2},{1,3},{2,0},{3,1},{4,6},{5,7},{6,4},{7,5},{8,10},{9,11},{10,... | collective-permute-start | bytes 511496 | tf_op jit(solution)/shard_map/ppermute | solution.py:27
  13.4 7.3 %collective-permute-start = (f32[72,296]{1,0:T(8,128)}, f32[72,296]{1,0:T(8,128)S(1)}, u32[]{:S(2)}, u32[]{:S(2)}) collective-permute-start(f32[72,296]{1,0:T(8,128)} %param.6), channel_id=1, source_target_pairs={{0,2},{1,3},{2,0},{3,1},{4,6},{5,7},{6,4},{7,5},{8,10},{9,11},{10,... | collective-permute-start | bytes 255752 | tf_op jit(solution)/shard_map/ppermute | solution.py:27
  13.5 3.1 %copy-start = (f32[16,296,296]{2,1,0:T(8,128)S(1)}, f32[16,296,296]{2,1,0:T(8,128)}, u32[]{:S(2)}) copy-start(f32[16,296,296]{2,1,0:T(8,128)} %op_ref.1) | copy-start | bytes 16822276
  19.5 2.7 %collective-permute-start.5 = (f32[288,296]{1,0:T(8,128)S(1)}, f32[288,296]{1,0:T(8,128)S(1)}, u32[]{:S(2)}, u32[]{:S(2)}) collective-permute-start(f32[288,296]{1,0:T(8,128)S(1)} %constant_dynamic-update-slice_fusion.2.near_ref), channel_id=1, source_target_pairs={{0,1},{1,0},{2,3},{3,2},{4,5},{5,4},{6,7},{7,6},{8,9},{9,8},{10,11... | collective-permute-start | bytes 1022984 | tf_op jit(solution)/shard_map/ppermute | solution.py:27
  20.7 1.5 %collective-permute-start.1 = (f32[144,296]{1,0:T(8,128)S(1)}, f32[144,296]{1,0:T(8,128)S(1)}, u32[]{:S(2)}, u32[]{:S(2)}) collective-permute-start(f32[144,296]{1,0:T(8,128)S(1)} %constant_dynamic-update-slice_fusion.own_ref), channel_id=1, source_target_pairs={{0,1},{1,0},{2,3},{3,2},{4,5},{5,4},{6,7},{7,6},{8,9},{9,8},{10,11... | collective-permute-start | bytes 511496 | tf_op jit(solution)/shard_map/ppermute | solution.py:27
  32.2 1.9 %collective-permute-start.6 = (f32[288,296]{1,0:T(8,128)S(1)}, f32[288,296]{1,0:T(8,128)S(1)}, u32[]{:S(2)}, u32[]{:S(2)}) collective-permute-start(f32[288,296]{1,0:T(8,128)S(1)} %get-tuple-element.25), channel_id=1, source_target_pairs={{0,1},{1,0},{2,3},{3,2},{4,5},{5,4},{6,7},{7,6},{8,9},{9,8},{10,11... | collective-permute-start | bytes 1022984 | tf_op jit(solution)/shard_map/ppermute | solution.py:27
  34.2 7.2 %collective-permute-start.7 = (f32[72,296]{1,0:T(8,128)S(1)}, f32[72,296]{1,0:T(8,128)S(1)}, u32[]{:S(2)}, u32[]{:S(2)}) collective-permute-start(f32[72,296]{1,0:T(8,128)S(1)} %get-tuple-element.27), channel_id=1, source_target_pairs={{0,4},{4,8},{8,12},{12,16},{16,20},{20,24},{24,28},{1,5},{5,9},{9,... | collective-permute-start | bytes 255752 | tf_op jit(solution)/shard_map/ppermute | solution.py:31
  38.7 6.7 %collective-permute-start.8 = (f32[72,296]{1,0:T(8,128)S(1)}, f32[72,296]{1,0:T(8,128)S(1)}, u32[]{:S(2)}, u32[]{:S(2)}) collective-permute-start(f32[72,296]{1,0:T(8,128)S(1)} %get-tuple-element.28), channel_id=1, source_target_pairs={{4,0},{8,4},{12,8},{16,12},{20,16},{24,20},{28,24},{5,1},{9,5},{13... | collective-permute-start | bytes 255752 | tf_op jit(solution)/shard_map/ppermute | solution.py:31
  45.6 4.8 %collective-permute-start.9 = (f32[72,296]{1,0:T(8,128)S(1)}, f32[72,296]{1,0:T(8,128)S(1)}, u32[]{:S(2)}, u32[]{:S(2)}) collective-permute-start(f32[72,296]{1,0:T(8,128)S(1)} %broadcast_select_fusion), channel_id=1, source_target_pairs={{0,2},{1,3},{2,0},{3,1},{4,6},{5,7},{6,4},{7,5},{8,10},{9,11},{10,... | collective-permute-start | bytes 255752 | tf_op jit(solution)/shard_map/ppermute | solution.py:27

commit v3 on v2

--- a/solution.py
+++ b/solution.py
@@ -10,7 +10,7 @@
 
 LANES = 128
 GRANT = 20 << 20
-BATCH = 2
+BATCH = 4
 
 
 def padded(size, to=LANES):
@@ -51,10 +51,74 @@
     )
 
 
-def operator_kernel(op_ref, main_ref, rest_ref, *, size, whole, room):
+def prepare_kernel(
+    owner_hbm,
+    group_hbm,
+    target_hbm,
+    source_hbm,
+    op_hbm,
+    pick_ref,
+    side_ref,
+    main_ref,
+    rest_ref,
+    owner_ref,
+    group_ref,
+    target_ref,
+    source_ref,
+    op_ref,
+    list_sem,
+    op_sem,
+    *,
+    boxes,
+    capacity,
+    quarter,
+    span,
+    whole,
+    room,
+):
+    offsets, size, _ = op_ref.shape
     tail = size - whole
+    lists = [
+        pltpu.make_async_copy(source, target, list_sem.at[i])
+        for i, (source, target) in enumerate(
+            (
+                (target_hbm, target_ref),
+                (source_hbm, source_ref),
+                (owner_hbm, owner_ref),
+                (group_hbm, group_ref),
+            )
+        )
+    ]
+
+    def fetch(k):
+        return pltpu.make_async_copy(op_hbm.at[k], op_ref.at[k], op_sem.at[k])
+
+    for copy in lists:
+        copy.start()
+    for k in range(offsets):
+        fetch(k).start()
+    for copy in lists:
+        copy.wait()
+
+    box = lax.axis_index("box")
+    core = lax.axis_index("op") % 2
+    starts, _, group_start = places(owner_ref, group_ref, box, boxes, capacity)
+    first = group_start - capacity // 3
+    found = jnp.where(target_ref[0] < capacity, source_ref[0] - first, -1)
+    found = jnp.concatenate(
+        [found, jnp.full((offsets, padded(capacity) - capacity), -1, jnp.int32)], axis=1
+    )
+    columns = found.T
+    row = lax.broadcasted_iota(jnp.int32, (capacity, span), 1)
+    for k in range(offsets):
+        hit = columns[:capacity, k : k + 1] == row
+        pick_ref[k] = jnp.where(hit, 1.0, 0.0).astype(jnp.bfloat16)
+    bound = group_start + group_ref[box] - starts[1]
+    slot = quarter * core + lax.broadcasted_iota(jnp.int32, side_ref.shape, 0)
+    side_ref[...] = jnp.where(slot >= bound, 1.0, 0.0)
 
     def split(k, carry):
+        fetch(k).wait()
         block = op_ref[k]
         high = block.astype(jnp.bfloat16)
         wide = high.astype(jnp.float32)
@@ -69,80 +133,63 @@
         main_ref[k, :, whole : 2 * whole] = low[:whole]
         main_ref[k, :, 2 * whole :] = ends[:whole]
         blank = jnp.zeros((room - tail, whole), jnp.bfloat16)
-        first = jnp.concatenate([high[whole:, :whole], blank], axis=0)
-        rest_ref[k, :room, :whole] = first
-        rest_ref[k, :room, whole : 2 * whole] = first
+        top = jnp.concatenate([high[whole:, :whole], blank], axis=0)
+        rest_ref[k, :room, :whole] = top
+        rest_ref[k, :room, whole : 2 * whole] = top
         rest_ref[k, :room, 2 * whole :] = jnp.concatenate([ends[whole:], blank[:, :LANES]], axis=0)
         rest_ref[k, room:, :whole] = jnp.concatenate([low[whole:], blank], axis=0)
         rest_ref[k, room:, whole:] = jnp.zeros((room, whole + LANES), jnp.bfloat16)
         return carry
 
-    lax.fori_loop(0, op_ref.shape[0], split, 0)
-
-
-def split_operators(operators):
-    count, size, _ = operators.shape
+    lax.fori_loop(0, offsets, split, 0)
+
+
+def prepare(owner_count, group_count, target_slot, source_box, operators, boxes, quarter, span):
+    _, offsets, capacity = target_slot.shape
+    size = operators.shape[1]
     whole = size // LANES * LANES
     room = padded(size - whole, 16)
     width = 2 * whole + LANES
+    hbm = pl.BlockSpec(memory_space=pltpu.HBM)
     vmem = pl.BlockSpec(memory_space=pltpu.VMEM)
     return pl.pallas_call(
-        functools.partial(operator_kernel, size=size, whole=whole, room=room),
-        in_specs=[vmem],
-        out_specs=[vmem, vmem],
+        functools.partial(
+            prepare_kernel,
+            boxes=boxes,
+            capacity=capacity,
+            quarter=quarter,
+            span=span,
+            whole=whole,
+            room=room,
+        ),
+        in_specs=[hbm] * 5,
+        out_specs=[vmem] * 4,
         out_shape=[
-            jax.ShapeDtypeStruct((count, whole, width), jnp.bfloat16),
-            jax.ShapeDtypeStruct((count, 2 * room, width), jnp.bfloat16),
+            jax.ShapeDtypeStruct((offsets, capacity, span), jnp.bfloat16),
+            jax.ShapeDtypeStruct((quarter, LANES), jnp.float32),
+            jax.ShapeDtypeStruct((offsets, whole, width), jnp.bfloat16),
+            jax.ShapeDtypeStruct((offsets, 2 * room, width), jnp.bfloat16),
+        ],
+        scratch_shapes=[
+            pltpu.SMEM(owner_count.shape, jnp.int32),
+            pltpu.SMEM(group_count.shape, jnp.int32),
+            pltpu.VMEM(target_slot.shape, jnp.int32),
+            pltpu.VMEM(source_box.shape, jnp.int32),
+            pltpu.VMEM(operators.shape, jnp.float32),
+            pltpu.SemaphoreType.DMA((4,)),
+            pltpu.SemaphoreType.DMA((offsets,)),
         ],
         compiler_params=pltpu.CompilerParams(vmem_limit_bytes=GRANT),
         cost_estimate=pl.CostEstimate(
-            flops=0, transcendentals=0, bytes_accessed=count * size * (4 * size + 2 * width)
+            flops=0, transcendentals=0, bytes_accessed=4 * offsets * size * size
         ),
-        name="split_operators",
-    )(operators)
-
-
-def select_kernel(owner_ref, group_ref, target_ref, source_ref, out_ref, side_ref, *, boxes, capacity, quarter, span):
-    box = lax.axis_index("box")
-    core = lax.axis_index("op") % 2
-    starts, _, group_start = places(owner_ref, group_ref, box, boxes, capacity)
-    first = group_start - capacity // 3
-    alive = target_ref[0] < capacity
-    found = jnp.where(alive, source_ref[0] - first, -1)
-    offsets = found.shape[0]
-    found = jnp.concatenate(
-        [found, jnp.full((offsets, padded(capacity) - capacity), -1, jnp.int32)], axis=1
-    )
-    columns = found.T
-    row = lax.broadcasted_iota(jnp.int32, (capacity, span), 1)
-    for k in range(offsets):
-        hit = columns[:capacity, k : k + 1] == row
-        out_ref[k] = jnp.where(hit, 1.0, 0.0).astype(jnp.bfloat16)
-    tail = group_start + group_ref[box] - starts[1]
-    slot = quarter * core + lax.broadcasted_iota(jnp.int32, side_ref.shape, 0)
-    side_ref[...] = jnp.where(slot >= tail, 1.0, 0.0)
-
-
-def selections(owner_count, group_count, target_slot, source_box, boxes, quarter, span):
-    _, offsets, capacity = target_slot.shape
-    smem = pl.BlockSpec(memory_space=pltpu.SMEM)
-    vmem = pl.BlockSpec(memory_space=pltpu.VMEM)
-    return pl.pallas_call(
-        functools.partial(
-            select_kernel, boxes=boxes, capacity=capacity, quarter=quarter, span=span
-        ),
-        in_specs=[smem, smem, vmem, vmem],
-        out_specs=[vmem, vmem],
-        out_shape=[
-            jax.ShapeDtypeStruct((offsets, capacity, span), jnp.bfloat16),
-            jax.ShapeDtypeStruct((quarter, LANES), jnp.float32),
-        ],
-        compiler_params=pltpu.CompilerParams(vmem_limit_bytes=GRANT),
-        cost_estimate=pl.CostEstimate(
-            flops=0, transcendentals=0, bytes_accessed=2 * offsets * capacity * span
-        ),
-        name="selections",
-    )(owner_count, group_count, target_slot, source_box)
+        name="prepare",
+    )(
+        *(
+            pltpu.with_memory_space_constraint(value, pltpu.HBM)
+            for value in (owner_count, group_count, target_slot, source_box, operators)
+        )
+    )
 
 
 def translate_kernel(
@@ -324,16 +371,17 @@
     earlier = to_box(density, 1)
     later = to_box(density, -1)
     across = flip(density, 2)
-    picks, side = selections(
-        owner_count, group_count, target_slot, source_box, boxes, quarter, span
-    )
     near = jnp.concatenate([earlier, later], axis=0)
-    near, picks = lax.optimization_barrier((near, picks))
+    own = jnp.concatenate([density, across], axis=0)
+    near, own = lax.optimization_barrier((near, own))
     near_across = flip(near, 2)
-    own = jnp.concatenate([density, across], axis=0)
     own_peer = flip(own, 1)
-    weights, rests = split_operators(operators)
-    near_across, weights, rests = lax.optimization_barrier((near_across, weights, rests))
+    picks, side, weights, rests = prepare(
+        owner_count, group_count, target_slot, source_box, operators, boxes, quarter, span
+    )
+    near_across, own_peer, picks, weights, rests = lax.optimization_barrier(
+        (near_across, own_peer, picks, weights, rests)
+    )
     near = jnp.concatenate([near, near_across], axis=0)
     near_peer = flip(near, 1)
     send, keep = translate(

time: 51.5 us -> 51.1 us (level)
  local copies, waits for them, and re-layouts: 5.92 us -> 0.06 us
  waiting for transfers between devices: 13.3 us -> 15.8 us
  Pallas kernels: 14 us -> 16.4 us
  other arithmetic: 1.01 us -> 1.96 us
    unnamed x18 -> x5, local copies, waits for them, and re-layouts: 5.88 us -> 0.02 us
    ppermute x4, waiting for transfers between devices: 5.31 us -> 8.49 us  [to_box(): return lax.ppermute(block, 'box', shifted('box', step))]
    pallas_call x2 -> x1, Pallas kernels: 4.03 us -> 6.89 us  [prepare(): pl.pallas_call(functools.partial(prepare_kernel, boxes=boxes, capacity=ca...]
    ppermute x4, starting transfers between devices: 12.7 us -> 11.4 us  [to_box(): return lax.ppermute(block, 'box', shifted('box', step))]
    ppermute x6, starting transfers between devices: 4.02 us -> 5.16 us  [flip(): return lax.ppermute(block, 'op', [(i, i ^ bit) for i in range(count)])]
    concatenate x0 -> x1, other arithmetic: none -> 0.95 us  [body(): own = jnp.concatenate([density, across], axis=0)]
    ppermute x6, waiting for transfers between devices: 8 us -> 7.31 us  [flip(): return lax.ppermute(block, 'op', [(i, i ^ bit) for i in range(count)])]
  transfers between devices with their start and end apart: 10 -> 10, of which waited for: 7 -> 7; matrix products, arithmetic and copies ran while one was open for 0% -> 2% of each run, Pallas kernels for 8% -> 14%
where the time goes in v3:
time: 51.1 us; the launch traced here: 50.9 us
  starting transfers between devices  16.6 us (32%)
  Pallas kernels  16.4 us (32%)
  waiting for transfers between devices  15.8 us (31%)
  other arithmetic  1.96 us (4%)
    ppermute x4, starting transfers between devices, to_box(): return lax.ppermute(block, 'box', shifted('box', step))  11.4 us
    pallas_call x1, Pallas kernels, translate(): pl.pallas_call(functools.partial(translate_kernel, boxes=boxes, capacity=...  9.48 us
    ppermute x4, waiting for transfers between devices, to_box(): return lax.ppermute(block, 'box', shifted('box', step))  8.49 us
    ppermute x6, waiting for transfers between devices, flip(): return lax.ppermute(block, 'op', [(i, i ^ bit) for i in range(count)])  7.31 us
    pallas_call x1, Pallas kernels, prepare(): pl.pallas_call(functools.partial(prepare_kernel, boxes=boxes, capacity=ca...  6.89 us
    ppermute x6, starting transfers between devices, flip(): return lax.ppermute(block, 'op', [(i, i ^ bit) for i in range(count)])  5.16 us
  transfers between devices with their start and end apart: 10, of which 7 were waited for; matrix products, arithmetic and copies ran while one was open for 2% of the time, Pallas kernels for 14%

profile of v3, /device:TPU:0, one launch (start us, length us, event | category | flops | bytes accessed | tf_op | source)
XLA Modules:
  0.0 50.9 jit_solution(797515583705341230)
XLA Ops:
  0.0 0.0 copy-start.1
  0.0 0.0 copy-start
  0.0 3.0 %collective-permute-start.2 = (f32[72,296]{1,0:T(8,128)}, f32[72,296]{1,0:T(8,128)S(1)}, u32[]{:S(2)}, u32[]{:S(2)}) collective-permute-start(f32[72,296]{1,0:T(8,128)} %param.6), channel_id=1, source_target_pairs={{0,2},{1,3},{2,0},{3,1},{4,6},{5,7},{6,4},{7,5},{8,10},{9,11},{10,... | collective-permute-start | bytes 255752 | tf_op jit(solution)/shard_map/ppermute | solution.py:27
  3.0 1.3 %collective-permute-start.1 = (f32[72,296]{1,0:T(8,128)}, f32[72,296]{1,0:T(8,128)S(1)}, u32[]{:S(2)}, u32[]{:S(2)}) collective-permute-start(f32[72,296]{1,0:T(8,128)} %param.6), channel_id=1, source_target_pairs={{4,0},{8,4},{12,8},{16,12},{20,16},{24,20},{28,24},{5,1},{9,5},{13... | collective-permute-start | bytes 255752 | tf_op jit(solution)/shard_map/ppermute | solution.py:31
  4.3 4.6 %collective-permute-start = (f32[72,296]{1,0:T(8,128)}, f32[72,296]{1,0:T(8,128)S(1)}, u32[]{:S(2)}, u32[]{:S(2)}) collective-permute-start(f32[72,296]{1,0:T(8,128)} %param.6), channel_id=1, source_target_pairs={{0,4},{4,8},{8,12},{12,16},{16,20},{20,24},{24,28},{1,5},{5,9},{9,... | collective-permute-start | bytes 255752 | tf_op jit(solution)/shard_map/ppermute | solution.py:31
  8.8 0.0 collective-permute-done.2
  8.8 0.9 %pad_maximum_fusion.1.own_ref = f32[144,296]{1,0:T(8,128)S(1)} fusion(f32[72,296]{1,0:T(8,128)S(1)} %collective-permute-done.2, f32[72,296]{1,0:T(8,128)} %param.6), kind=kLoop, calls=%fused_computation.1 | loop fusion | flops 42624 | bytes 340992 | tf_op jit(solution)/shard_map/concatenate | solution.py:375
  9.8 0.0 collective-permute-done.1
  9.8 2.2 %collective-permute-done = f32[72,296]{1,0:T(8,128)S(1)} collective-permute-done((f32[72,296]{1,0:T(8,128)}, f32[72,296]{1,0:T(8,128)S(1)}, u32[]{:S(2)}, u32[]{:S(2)}) %collective-permute-start) | collective-permute-done | bytes 85280 | tf_op jit(solution)/shard_map/ppermute | solution.py:31
  12.1 0.1 collective-permute-start.4
  12.2 0.5 %collective-permute-start.3 = (f32[144,296]{1,0:T(8,128)S(1)}, f32[144,296]{1,0:T(8,128)S(1)}, u32[]{:S(2)}, u32[]{:S(2)}) collective-permute-start(f32[144,296]{1,0:T(8,128)S(1)} %pad_maximum_fusion), channel_id=1, source_target_pairs={{0,2},{1,3},{2,0},{3,1},{4,6},{5,7},{6,4},{7,5},{8,10},{9,11},{10,... | collective-permute-start | bytes 511496 | tf_op jit(solution)/shard_map/ppermute | solution.py:27
  12.7 6.9 %prepare.1 = (bf16[16,288,512]{2,1,0:T(8,128)(2,1)S(1)}, f32[72,128]{1,0:T(8,128)S(1)}, bf16[16,256,640]{2,1,0:T(8,128)(2,1)S(1)}, bf16[16,96,640]{2,1,0:T(8,128)(2,1)S(1)}) custom-call(s32[8]{0:T(128)} %owner_ref.1, s32[8]{0:T(128)} %group_ref.1, s32[1,16,288]{2,1,0:T(8,128)} %target_hbm.1, s32[1,16,288]{2,1,0:T(8,128)} %source_hbm.1, f32[16,296,296]{2,1,0:T(8,128)} %op_hbm.1), custom_call_target="tpu_custom_call" | custom-call | bytes 5607424 | tf_op jit(solution)/shard_map/prepare/pallas_call | solution.py:155
  19.6 0.0 collective-permute-done.4.own_peer_ref
  19.6 0.4 collective-permute-done.3
  20.0 0.1 collective-permute-start.5
  20.1 1.8 %collective-permute-done.5.near_peer_ref = f32[288,296]{1,0:T(8,128)S(1)} collective-permute-done((f32[288,296]{1,0:T(8,128)S(1)}, f32[288,296]{1,0:T(8,128)S(1)}, u32[]{:S(2)}, u32[]{:S(2)}) %collective-permute-start.5) | collective-permute-done | bytes 341024 | tf_op jit(solution)/shard_map/ppermute | solution.py:27
  21.9 0.0 copy-done.1
  21.9 0.0 copy-done
  21.9 9.5 %translate.1 = (f32[288,296]{1,0:T(8,128)S(1)}, f32[288,296]{1,0:T(8,128)S(1)}) custom-call(s32[8]{0:T(128)S(1)} %copy-done, s32[8]{0:T(128)S(1)} %copy-done.1, f32[144,296]{1,0:T(8,128)S(1)} %pad_maximum_fusion.1.own_ref, f32[144,296]{1,0:T(8,128)S(1)} %collective-permute-done.4.own_peer_ref, f32[288,296]{1,0:T(8,128)S(1)} %constant_dynamic-update-slice_fusion.near_ref, ...), custom_call_target="tpu_custom_call" | custom-call | tf_op jit(solution)/shard_map/translate/pallas_call | solution.py:336
  31.4 0.2 collective-permute-start.6
  31.6 1.7 %collective-permute-done.6 = f32[288,296]{1,0:T(8,128)S(1)} collective-permute-done((f32[288,296]{1,0:T(8,128)S(1)}, f32[288,296]{1,0:T(8,128)S(1)}, u32[]{:S(2)}, u32[]{:S(2)}) %collective-permute-start.6) | collective-permute-done | bytes 341024 | tf_op jit(solution)/shard_map/ppermute | solution.py:27
  33.3 4.3 %collective-permute-start.7 = (f32[72,296]{1,0:T(8,128)S(1)}, f32[72,296]{1,0:T(8,128)S(1)}, u32[]{:S(2)}, u32[]{:S(2)}) collective-permute-start(f32[72,296]{1,0:T(8,128)S(1)} %get-tuple-element.31), channel_id=1, source_target_pairs={{0,4},{4,8},{8,12},{12,16},{16,20},{20,24},{24,28},{1,5},{5,9},{9,... | collective-permute-start | bytes 255752 | tf_op jit(solution)/shard_map/ppermute | solution.py:31
  37.6 1.3 %collective-permute-start.8 = (f32[72,296]{1,0:T(8,128)S(1)}, f32[72,296]{1,0:T(8,128)S(1)}, u32[]{:S(2)}, u32[]{:S(2)}) collective-permute-start(f32[72,296]{1,0:T(8,128)S(1)} %get-tuple-element.32), channel_id=1, source_target_pairs={{4,0},{8,4},{12,8},{16,12},{20,16},{24,20},{28,24},{5,1},{9,5},{13... | collective-permute-start | bytes 255752 | tf_op jit(solution)/shard_map/ppermute | solution.py:31
  38.9 0.1 fusion.1
  39.0 1.2 %collective-permute-done.7 = f32[72,296]{1,0:T(8,128)S(1)} collective-permute-done((f32[72,296]{1,0:T(8,128)S(1)}, f32[72,296]{1,0:T(8,128)S(1)}, u32[]{:S(2)}, u32[]{:S(2)}) %collective-permute-start.7) | collective-permute-done | bytes 85280 | tf_op jit(solution)/shard_map/ppermute | solution.py:31
  40.2 5.0 %collective-permute-done.8 = f32[72,296]{1,0:T(8,128)S(1)} collective-permute-done((f32[72,296]{1,0:T(8,128)S(1)}, f32[72,296]{1,0:T(8,128)S(1)}, u32[]{:S(2)}, u32[]{:S(2)}) %collective-permute-start.8) | collective-permute-done | bytes 85280 | tf_op jit(solution)/shard_map/ppermute | solution.py:31
  45.2 0.1 broadcast_select_fusion
  45.3 1.3 %collective-permute-start.9 = (f32[72,296]{1,0:T(8,128)S(1)}, f32[72,296]{1,0:T(8,128)S(1)}, u32[]{:S(2)}, u32[]{:S(2)}) collective-permute-start(f32[72,296]{1,0:T(8,128)S(1)} %broadcast_select_fusion), channel_id=1, source_target_pairs={{0,2},{1,3},{2,0},{3,1},{4,6},{5,7},{6,4},{7,5},{8,10},{9,11},{10,... | collective-permute-start | bytes 255752 | tf_op jit(solution)/shard_map/ppermute | solution.py:27
  46.6 3.5 %collective-permute-done.9 = f32[72,296]{1,0:T(8,128)S(1)} collective-permute-done((f32[72,296]{1,0:T(8,128)S(1)}, f32[72,296]{1,0:T(8,128)S(1)}, u32[]{:S(2)}, u32[]{:S(2)}) %collective-permute-start.9) | collective-permute-done | bytes 85280 | tf_op jit(solution)/shard_map/ppermute | solution.py:27
  50.1 0.7 %select_add_fusion = f32[72,296]{1,0:T(8,128)} fusion(f32[72,296]{1,0:T(8,128)S(1)} %collective-permute-done.9, pred[]{:T(512)S(6)} %lt.3, f32[72,296]{1,0:T(8,128)S(1)} %collective-permute-done.8, pred[72]{0:T(512)(128)(4,1)S(1)} %fusion.1, f32[288,296]{1,0:T(8,128)S(1)} %add.15, f32[72,296]{1,0:T(8,128)S(1)} %collective-permute-done.7), kind=kLoop, calls=%fused_computation.5 | loop fusion | flops 149184 | bytes 511561 | tf_op jit(solution)/shard_map/add | solution.py:398
  (5 shorter events, 0.1 us)
Async XLA Ops:
  0.0 21.9 %copy-start.1 = (s32[8]{0:T(128)S(1)}, s32[8]{0:T(128)}, u32[]{:S(2)}) copy-start(s32[8]{0:T(128)} %group_ref.1) | copy-start | bytes 100
  0.0 21.9 %copy-start = (s32[8]{0:T(128)S(1)}, s32[8]{0:T(128)}, u32[]{:S(2)}) copy-start(s32[8]{0:T(128)} %owner_ref.1) | copy-start | bytes 100
  0.0 8.8 %collective-permute-start.2 = (f32[72,296]{1,0:T(8,128)}, f32[72,296]{1,0:T(8,128)S(1)}, u32[]{:S(2)}, u32[]{:S(2)}) collective-permute-start(f32[72,296]{1,0:T(8,128)} %param.6), channel_id=1, source_target_pairs={{0,2},{1,3},{2,0},{3,1},{4,6},{5,7},{6,4},{7,5},{8,10},{9,11},{10,... | collective-permute-start | bytes 255752 | tf_op jit(solution)/shard_map/ppermute | solution.py:27
  3.0 6.8 %collective-permute-start.1 = (f32[72,296]{1,0:T(8,128)}, f32[72,296]{1,0:T(8,128)S(1)}, u32[]{:S(2)}, u32[]{:S(2)}) collective-permute-start(f32[72,296]{1,0:T(8,128)} %param.6), channel_id=1, source_target_pairs={{4,0},{8,4},{12,8},{16,12},{20,16},{24,20},{28,24},{5,1},{9,5},{13... | collective-permute-start | bytes 255752 | tf_op jit(solution)/shard_map/ppermute | solution.py:31
  4.3 7.8 %collective-permute-start = (f32[72,296]{1,0:T(8,128)}, f32[72,296]{1,0:T(8,128)S(1)}, u32[]{:S(2)}, u32[]{:S(2)}) collective-permute-start(f32[72,296]{1,0:T(8,128)} %param.6), channel_id=1, source_target_pairs={{0,4},{4,8},{8,12},{12,16},{16,20},{20,24},{24,28},{1,5},{5,9},{9,... | collective-permute-start | bytes 255752 | tf_op jit(solution)/shard_map/ppermute | solution.py:31
  12.1 7.5 %collective-permute-start.4 = (f32[144,296]{1,0:T(8,128)S(1)}, f32[144,296]{1,0:T(8,128)S(1)}, u32[]{:S(2)}, u32[]{:S(2)}) collective-permute-start(f32[144,296]{1,0:T(8,128)S(1)} %pad_maximum_fusion.1.own_ref), channel_id=1, source_target_pairs={{0,1},{1,0},{2,3},{3,2},{4,5},{5,4},{6,7},{7,6},{8,9},{9,8},{10,11... | collective-permute-start | bytes 511496 | tf_op jit(solution)/shard_map/ppermute | solution.py:27
  12.2 7.8 %collective-permute-start.3 = (f32[144,296]{1,0:T(8,128)S(1)}, f32[144,296]{1,0:T(8,128)S(1)}, u32[]{:S(2)}, u32[]{:S(2)}) collective-permute-start(f32[144,296]{1,0:T(8,128)S(1)} %pad_maximum_fusion), channel_id=1, source_target_pairs={{0,2},{1,3},{2,0},{3,1},{4,6},{5,7},{6,4},{7,5},{8,10},{9,11},{10,... | collective-permute-start | bytes 511496 | tf_op jit(solution)/shard_map/ppermute | solution.py:27
  20.0 1.9 %collective-permute-start.5 = (f32[288,296]{1,0:T(8,128)S(1)}, f32[288,296]{1,0:T(8,128)S(1)}, u32[]{:S(2)}, u32[]{:S(2)}) collective-permute-start(f32[288,296]{1,0:T(8,128)S(1)} %constant_dynamic-update-slice_fusion.near_ref), channel_id=1, source_target_pairs={{0,1},{1,0},{2,3},{3,2},{4,5},{5,4},{6,7},{7,6},{8,9},{9,8},{10,11... | collective-permute-start | bytes 1022984 | tf_op jit(solution)/shard_map/ppermute | solution.py:27
  31.4 1.9 %collective-permute-start.6 = (f32[288,296]{1,0:T(8,128)S(1)}, f32[288,296]{1,0:T(8,128)S(1)}, u32[]{:S(2)}, u32[]{:S(2)}) collective-permute-start(f32[288,296]{1,0:T(8,128)S(1)} %get-tuple-element.29), channel_id=1, source_target_pairs={{0,1},{1,0},{2,3},{3,2},{4,5},{5,4},{6,7},{7,6},{8,9},{9,8},{10,11... | collective-permute-start | bytes 1022984 | tf_op jit(solution)/shard_map/ppermute | solution.py:27
  33.3 6.9 %collective-permute-start.7 = (f32[72,296]{1,0:T(8,128)S(1)}, f32[72,296]{1,0:T(8,128)S(1)}, u32[]{:S(2)}, u32[]{:S(2)}) collective-permute-start(f32[72,296]{1,0:T(8,128)S(1)} %get-tuple-element.31), channel_id=1, source_target_pairs={{0,4},{4,8},{8,12},{12,16},{16,20},{20,24},{24,28},{1,5},{5,9},{9,... | collective-permute-start | bytes 255752 | tf_op jit(solution)/shard_map/ppermute | solution.py:31
  37.6 7.6 %collective-permute-start.8 = (f32[72,296]{1,0:T(8,128)S(1)}, f32[72,296]{1,0:T(8,128)S(1)}, u32[]{:S(2)}, u32[]{:S(2)}) collective-permute-start(f32[72,296]{1,0:T(8,128)S(1)} %get-tuple-element.32), channel_id=1, source_target_pairs={{4,0},{8,4},{12,8},{16,12},{20,16},{24,20},{28,24},{5,1},{9,5},{13... | collective-permute-start | bytes 255752 | tf_op jit(solution)/shard_map/ppermute | solution.py:31
  45.3 4.8 %collective-permute-start.9 = (f32[72,296]{1,0:T(8,128)S(1)}, f32[72,296]{1,0:T(8,128)S(1)}, u32[]{:S(2)}, u32[]{:S(2)}) collective-permute-start(f32[72,296]{1,0:T(8,128)S(1)} %broadcast_select_fusion), channel_id=1, source_target_pairs={{0,2},{1,3},{2,0},{3,1},{4,6},{5,7},{6,4},{7,5},{8,10},{9,11},{10,... | collective-permute-start | bytes 255752 | tf_op jit(solution)/shard_map/ppermute | solution.py:27

commit v4 on v3

v4 whole, which is shorter than its diff:
```python
import functools
import math

import jax
import jax.numpy as jnp
from jax import lax
from jax.experimental import pallas as pl
from jax.experimental.pallas import tpu as pltpu
from jax.sharding import PartitionSpec as P

LANES = 128
GRANT = 20 << 20
BATCH = 2


def padded(size, to=LANES):
    return -(-size // to) * to


def shifted(pairs_axis, step):
    count = lax.axis_size(pairs_axis)
    return [(i, i + step) for i in range(count) if 0 <= i + step < count]


def flip(block, bit):
    count = lax.axis_size("op")
    return lax.ppermute(block, "op", [(i, i ^ bit) for i in range(count)])


def to_box(block, step):
    return lax.ppermute(block, "box", shifted("box", step))


def prefix(count_ref, upto):
    return lax.fori_loop(0, upto, lambda i, total: total + count_ref[i], 0)


def places(owner_ref, group_ref, box, boxes, capacity):
    before = jnp.maximum(box - 1, 0)
    after = jnp.minimum(box + 1, boxes - 1)
    own_start = prefix(owner_ref, box)
    own_count = owner_ref[box]
    prev_count = jnp.where(box > 0, owner_ref[before], 0)
    prev_start = own_start - jnp.where(box > 0, prev_count, capacity)
    next_start = own_start + own_count
    next_count = jnp.where(box < boxes - 1, owner_ref[after], 0)
    return (
        (prev_start, own_start, next_start),
        (prev_count, own_count, next_count),
        prefix(group_ref, box),
    )


def pinned(*values):
    return tuple(pltpu.with_memory_space_constraint(value, pltpu.HBM) for value in values)


def select_kernel(
    owner_hbm,
    group_hbm,
    target_hbm,
    source_hbm,
    pick_ref,
    side_ref,
    owner_ref,
    group_ref,
    target_ref,
    source_ref,
    sems,
    *,
    boxes,
    capacity,
    quarter,
    span,
):
    pairs = (
        (target_hbm, target_ref),
        (source_hbm, source_ref),
        (owner_hbm, owner_ref),
        (group_hbm, group_ref),
    )
    copies = [
        pltpu.make_async_copy(source, target, sems.at[i]) for i, (source, target) in enumerate(pairs)
    ]
    for copy in copies:
        copy.start()
    for copy in copies:
        copy.wait()
    box = lax.axis_index("box")
    core = lax.axis_index("op") % 2
    starts, _, group_start = places(owner_ref, group_ref, box, boxes, capacity)
    first = group_start - capacity // 3
    found = jnp.where(target_ref[0] < capacity, source_ref[0] - first, -1)
    offsets = found.shape[0]
    found = jnp.concatenate(
        [found, jnp.full((offsets, padded(capacity) - capacity), -1, jnp.int32)], axis=1
    )
    columns = found.T
    row = lax.broadcasted_iota(jnp.int32, (capacity, span), 1)
    for k in range(offsets):
        hit = columns[:capacity, k : k + 1] == row
        pick_ref[k] = jnp.where(hit, 1.0, 0.0).astype(jnp.bfloat16)
    bound = group_start + group_ref[box] - starts[1]
    slot = quarter * core + lax.broadcasted_iota(jnp.int32, side_ref.shape, 0)
    side_ref[...] = jnp.where(slot >= bound, 1.0, 0.0)


def selections(owner_count, group_count, target_slot, source_box, boxes, quarter, span):
    _, offsets, capacity = target_slot.shape
    hbm = pl.BlockSpec(memory_space=pltpu.HBM)
    vmem = pl.BlockSpec(memory_space=pltpu.VMEM)
    return pl.pallas_call(
        functools.partial(
            select_kernel, boxes=boxes, capacity=capacity, quarter=quarter, span=span
        ),
        in_specs=[hbm] * 4,
        out_specs=[vmem] * 2,
        out_shape=[
            jax.ShapeDtypeStruct((offsets, capacity, span), jnp.bfloat16),
            jax.ShapeDtypeStruct((quarter, LANES), jnp.float32),
        ],
        scratch_shapes=[
            pltpu.SMEM(owner_count.shape, jnp.int32),
            pltpu.SMEM(group_count.shape, jnp.int32),
            pltpu.VMEM(target_slot.shape, jnp.int32),
            pltpu.VMEM(source_box.shape, jnp.int32),
            pltpu.SemaphoreType.DMA((4,)),
        ],
        compiler_params=pltpu.CompilerParams(vmem_limit_bytes=GRANT),
        cost_estimate=pl.CostEstimate(
            flops=0, transcendentals=0, bytes_accessed=2 * offsets * capacity * span
        ),
        name="selections",
    )(*pinned(owner_count, group_count, target_slot, source_box))


def split_kernel(op_hbm, main_ref, rest_ref, op_ref, sems, *, whole, room):
    offsets, size, _ = op_ref.shape
    tail = size - whole

    def fetch(k):
        return pltpu.make_async_copy(op_hbm.at[k], op_ref.at[k], sems.at[k])

    for k in range(offsets):
        fetch(k).start()

    def split(k, carry):
        fetch(k).wait()
        block = op_ref[k]
        high = block.astype(jnp.bfloat16)
        wide = high.astype(jnp.float32)
        low = block - wide
        space = jnp.zeros((size, LANES - tail), jnp.float32)
        high_tail = jnp.concatenate([wide[:, whole:], space], axis=1)
        low_tail = jnp.concatenate([low[:, whole:], space], axis=1)
        ends = high_tail + pltpu.roll(high_tail, tail, 1) + pltpu.roll(low_tail, 2 * tail, 1)
        low = low[:, :whole].astype(jnp.bfloat16)
        ends = ends.astype(jnp.bfloat16)
        main_ref[k, :, :whole] = high[:whole, :whole]
        main_ref[k, :, whole : 2 * whole] = low[:whole]
        main_ref[k, :, 2 * whole :] = ends[:whole]
        blank = jnp.zeros((room - tail, whole), jnp.bfloat16)
        rest_ref[k, :room, :whole] = jnp.concatenate([high[whole:, :whole], blank], axis=0)
        rest_ref[k, room:, :whole] = jnp.concatenate([low[whole:], blank], axis=0)
        rest_ref[k, :room, whole:] = jnp.concatenate([ends[whole:], blank[:, :LANES]], axis=0)
        rest_ref[k, room:, whole:] = jnp.zeros((room, LANES), jnp.bfloat16)
        return carry

    lax.fori_loop(0, offsets, split, 0)


def split_operators(operators):
    offsets, size, _ = operators.shape
    whole = size // LANES * LANES
    room = padded(size - whole, 16)
    hbm = pl.BlockSpec(memory_space=pltpu.HBM)
    vmem = pl.BlockSpec(memory_space=pltpu.VMEM)
    return pl.pallas_call(
        functools.partial(split_kernel, whole=whole, room=room),
        in_specs=[hbm],
        out_specs=[vmem] * 2,
        out_shape=[
            jax.ShapeDtypeStruct((offsets, whole, 2 * whole + LANES), jnp.bfloat16),
            jax.ShapeDtypeStruct((offsets, 2 * room, whole + LANES), jnp.bfloat16),
        ],
        scratch_shapes=[
            pltpu.VMEM(operators.shape, jnp.float32),
            pltpu.SemaphoreType.DMA((offsets,)),
        ],
        compiler_params=pltpu.CompilerParams(vmem_limit_bytes=GRANT),
        cost_estimate=pl.CostEstimate(
            flops=0, transcendentals=0, bytes_accessed=4 * offsets * size * size
        ),
        name="split_operators",
    )(*pinned(operators))


def translate_kernel(
    owner_ref,
    group_ref,
    own_ref,
    near_ref,
    weight_ref,
    rest_ref,
    pick_ref,
    send_ref,
    keep_ref,
    window,
    packed,
    total,
    ends,
    *,
    boxes,
    capacity,
    quarter,
    size,
    span,
    need,
    batch,
):
    box = lax.axis_index("box")
    device = lax.axis_index("op")
    core = device % 2
    whole = size // LANES * LANES
    tail = size - whole
    third = capacity // 3
    tiles = padded(size) // LANES
    room = rest_ref.shape[1] // 2
    starts, counts, group_start = places(owner_ref, group_ref, box, boxes, capacity)

    def columns(tile):
        return slice(tile * LANES, min((tile + 1) * LANES, size))

    margin = 2 * third
    for owner in range(3):
        source, blocks = (own_ref, 1) if owner == 1 else (near_ref, 2)
        for part in range(4):
            at = margin + starts[owner] + quarter * part - (group_start - third)
            at = jnp.clip(at, 0, window.shape[1] - quarter)
            mask = device ^ part
            order = 2 * (mask % 2) + mask // 2
            line = pl.multiple_of(quarter * (blocks * order + (1 if owner == 2 else 0)), 8)
            for tile in range(tiles):
                lanes = columns(tile)
                window[tile, pl.ds(at, quarter), : lanes.stop - lanes.start] = source[
                    pl.ds(line, quarter), lanes
                ]

    def pack(index, carry):
        base = pl.multiple_of(index * LANES, LANES)
        inside = pl.ds(base, LANES)
        row = base + lax.broadcasted_iota(jnp.int32, (LANES, LANES), 0)
        lane = lax.broadcasted_iota(jnp.int32, (LANES, LANES), 1)
        for tile in range(tiles):
            fine = row < need
            if tile == tiles - 1:
                fine = fine & (lane < tail)
            value = jnp.where(fine, window[tile, pl.ds(margin + base, LANES), :], 0.0)
            high = value.astype(jnp.bfloat16)
            low = value - high.astype(jnp.float32)
            if tile < tiles - 1:
                packed[inside, tile * LANES : (tile + 1) * LANES] = high
                packed[inside, whole + tile * LANES : whole + (tile + 1) * LANES] = low.astype(
                    jnp.bfloat16
                )
            else:
                high = high.astype(jnp.float32)
                rest = high + pltpu.roll(low, tail, 1) + pltpu.roll(high, 2 * tail, 1)
                packed[inside, 2 * whole :] = rest.astype(jnp.bfloat16)
        return carry

    lax.fori_loop(0, span // LANES, pack, 0)
    total[:, capacity : 2 * capacity, :] = jnp.zeros((tiles, capacity, LANES), jnp.float32)
    ends[...] = jnp.zeros(ends.shape, jnp.float32)

    def product(left, right):
        return lax.dot_general(
            jnp.concatenate(left, axis=1),
            jnp.concatenate(right, axis=1),
            (((1,), (1,)), ((), ())),
            preferred_element_type=jnp.float32,
        )

    def offsets(index, carry):
        base = index * batch
        several = range(batch)
        picks = pick_ref[pl.ds(base, batch)].reshape(batch * capacity, span)
        picked = jnp.dot(picks, packed[...], preferred_element_type=jnp.float32).astype(jnp.bfloat16)
        rows = [picked[i * capacity : (i + 1) * capacity] for i in several]
        high = [value[:, :whole] for value in rows]
        last = [value[:, 2 * whole :] for value in rows]
        both = [jnp.concatenate([value[:, :whole], value[:, whole : 2 * whole]], axis=0) for value in rows]
        wide = product(both, [weight_ref[base + i, :, :whole] for i in several])
        part = wide[:capacity] + wide[capacity:]
        part += product(
            high + last,
            [weight_ref[base + i, :, whole : 2 * whole] for i in several]
            + [weight_ref[base + i, :, 2 * whole :] for i in several],
        )
        for tile in range(tiles - 1):
            total[tile, capacity : 2 * capacity, :] += part[:, tile * LANES : (tile + 1) * LANES]
        wide = product(both, [rest_ref[base + i, :, :whole] for i in several])
        ends[:, : 2 * room] += (
            wide[:capacity]
            + wide[capacity:]
            + product(last, [rest_ref[base + i, :, whole:] for i in several])
        )
        return carry

    lax.fori_loop(0, pick_ref.shape[0] // batch, offsets, 0)
    both = ends[...]
    total[tiles - 1, capacity : 2 * capacity, :] = both + pltpu.roll(both, LANES - room, 1)

    slot = lax.broadcasted_iota(jnp.int32, (quarter, LANES), 0)

    def place(ref, first, parts):
        spots = []
        for owner, block in parts:
            shift = starts[owner] - group_start + quarter * block
            low = jnp.maximum(-shift, 0)
            high = jnp.minimum(counts[owner] - quarter * block, capacity - shift)
            at = jnp.clip(capacity + shift, 0, total.shape[1] - quarter)
            spots.append((at, (slot >= low) & (slot < high)))
        for tile in range(tiles):
            lanes = columns(tile)
            value = sum(
                jnp.where(fine, total[tile, pl.ds(at, quarter), :], 0.0) for at, fine in spots
            )
            ref[first : first + quarter, lanes] = value[:, : lanes.stop - lanes.start]

    for ref, side in ((send_ref, 1 - core), (keep_ref, core)):
        place(ref, 0, [(1, side)])
        place(ref, quarter, [(1, side + 2)])
        place(ref, 2 * quarter, [(0, side), (0, side + 2)])
        place(ref, 3 * quarter, [(2, side)])


def translate(owner_count, group_count, own, near, weights, rests, picks, boxes):
    offsets, capacity, span = picks.shape
    size = own.shape[1]
    quarter = own.shape[0] // 4
    need = capacity + 2 * (capacity // 3)
    tiles = padded(size) // LANES
    smem = pl.BlockSpec(memory_space=pltpu.SMEM)
    vmem = pl.BlockSpec(memory_space=pltpu.VMEM)
    return pl.pallas_call(
        functools.partial(
            translate_kernel,
            boxes=boxes,
            capacity=capacity,
            quarter=quarter,
            size=size,
            span=span,
            need=need,
            batch=math.gcd(offsets, BATCH),
        ),
        in_specs=[smem, smem] + [vmem] * 5,
        out_specs=[vmem, vmem],
        out_shape=[jax.ShapeDtypeStruct((capacity, size), jnp.float32)] * 2,
        scratch_shapes=[
            pltpu.VMEM((tiles, 3 * capacity, LANES), jnp.float32),
            pltpu.VMEM((span, weights.shape[2]), jnp.bfloat16),
            pltpu.VMEM((tiles, 3 * capacity, LANES), jnp.float32),
            pltpu.VMEM((capacity, LANES), jnp.float32),
        ],
        compiler_params=pltpu.CompilerParams(vmem_limit_bytes=GRANT),
        name="translate",
    )(owner_count, group_count, own, near, weights, rests, picks)


def body(density, operators, owner_count, group_count, target_slot, source_box):
    quarter = density.shape[0]
    parts = lax.axis_size("op")
    boxes = lax.axis_size("box")
    capacity = quarter * parts
    if parts != 4:
        raise ValueError("unsupported op axis")
    span = padded(capacity + 2 * (capacity // 3))
    device = lax.axis_index("op")

    earlier = to_box(density, 1)
    later = to_box(density, -1)
    across = flip(density, 2)
    near = jnp.concatenate([earlier, later], axis=0)
    own = jnp.concatenate([density, across], axis=0)
    picks, side = selections(
        owner_count, group_count, target_slot, source_box, boxes, quarter, span
    )
    near, own, picks = lax.optimization_barrier((near, own, picks))
    near_across = flip(near, 2)
    own_peer = flip(own, 1)
    weights, rests = split_operators(operators)
    near_across, own_peer, weights, rests = lax.optimization_barrier(
        (near_across, own_peer, weights, rests)
    )
    own = jnp.concatenate([own, own_peer], axis=0)
    near = jnp.concatenate([near, near_across], axis=0)
    near = jnp.concatenate([near, flip(near, 1)], axis=0)
    send, keep = translate(owner_count, group_count, own, near, weights, rests, picks, boxes)
    both = keep + flip(send, 1)
    low, high, down, up = (both[i * quarter : (i + 1) * quarter] for i in range(4))
    from_after = to_box(down, -1)
    from_before = to_box(up, 1)
    early = side[:, :1] > 0.5
    low = low + from_before + jnp.where(early, from_after, 0.0)
    high = high + jnp.where(early, 0.0, from_after)
    first = device < 2
    return jnp.where(first, low, high) + flip(jnp.where(first, high, low), 2)


def solution(mesh):
    placed = (
        P(("box", "op"), None),
        P("op", None, None),
        P(),
        P(),
        P("box", "op", None),
        P("box", "op", None),
    )
    return jax.shard_map(
        body, mesh=mesh, in_specs=placed, out_specs=P(("box", "op"), None), check_vma=False
    )
```

time: 51.1 us -> 52 us (1.018)
  waiting for transfers between devices: 15.8 us -> 17.3 us
  starting transfers between devices: 16.6 us -> 15.9 us
    ppermute x6, waiting for transfers between devices: 7.31 us -> 10.7 us  [flip(): return lax.ppermute(block, 'op', [(i, i ^ bit) for i in range(count)])]
    ppermute x4, waiting for transfers between devices: 8.49 us -> 6.54 us  [to_box(): return lax.ppermute(block, 'box', shifted('box', step))]
    pallas_call x1 -> x2, Pallas kernels: 6.89 us -> 6.12 us  [the longest x1 4.15 us: split_operators(): pl.pallas_call(functools.partial(split_kernel, whole=whole, room=room), i...]
    pallas_call x1, Pallas kernels: 9.48 us -> 10.2 us  [translate(): pl.pallas_call(functools.partial(translate_kernel, boxes=boxes, capacity=...]
    ppermute x6, starting transfers between devices: 5.16 us -> 4.45 us  [flip(): return lax.ppermute(block, 'op', [(i, i ^ bit) for i in range(count)])]
  transfers between devices with their start and end apart: 10 -> 10, of which waited for: 7 -> 7; matrix products, arithmetic and copies ran while one was open for 2% -> 2% of each run, Pallas kernels for 14% -> 12%
where the time goes in v4:
time: 52 us; the launch traced here: 51.7 us
  waiting for transfers between devices  17.3 us (33%)
  Pallas kernels  16.3 us (31%)
  starting transfers between devices  15.9 us (31%)
  other arithmetic  2.05 us (4%)
    ppermute x4, starting transfers between devices, to_box(): return lax.ppermute(block, 'box', shifted('box', step))  11.4 us
    ppermute x6, waiting for transfers between devices, flip(): return lax.ppermute(block, 'op', [(i, i ^ bit) for i in range(count)])  10.7 us
    pallas_call x1, Pallas kernels, translate(): pl.pallas_call(functools.partial(translate_kernel, boxes=boxes, capacity=...  10.2 us
    ppermute x4, waiting for transfers between devices, to_box(): return lax.ppermute(block, 'box', shifted('box', step))  6.54 us
    ppermute x6, starting transfers between devices, flip(): return lax.ppermute(block, 'op', [(i, i ^ bit) for i in range(count)])  4.45 us
    pallas_call x1, Pallas kernels, split_operators(): pl.pallas_call(functools.partial(split_kernel, whole=whole, room=room), i...  4.15 us
    pallas_call x1, Pallas kernels, selections(): pl.pallas_call(functools.partial(select_kernel, boxes=boxes, capacity=cap...  1.97 us
  transfers between devices with their start and end apart: 10, of which 7 were waited for; matrix products, arithmetic and copies ran while one was open for 2% of the time, Pallas kernels for 12%

profile of v4, /device:TPU:0, one launch (start us, length us, event | category | flops | bytes accessed | tf_op | source)
XLA Modules:
  0.0 51.7 jit_solution(10065291867330315791)
XLA Ops:
  0.0 3.0 %collective-permute-start.2 = (f32[72,296]{1,0:T(8,128)}, f32[72,296]{1,0:T(8,128)S(1)}, u32[]{:S(2)}, u32[]{:S(2)}) collective-permute-start(f32[72,296]{1,0:T(8,128)} %param.6), channel_id=1, source_target_pairs={{0,2},{1,3},{2,0},{3,1},{4,6},{5,7},{6,4},{7,5},{8,10},{9,11},{10,... | collective-permute-start | bytes 255752 | tf_op jit(solution)/shard_map/ppermute | solution.py:27
  3.0 1.3 %collective-permute-start.1 = (f32[72,296]{1,0:T(8,128)}, f32[72,296]{1,0:T(8,128)S(1)}, u32[]{:S(2)}, u32[]{:S(2)}) collective-permute-start(f32[72,296]{1,0:T(8,128)} %param.6), channel_id=1, source_target_pairs={{4,0},{8,4},{12,8},{16,12},{20,16},{24,20},{28,24},{5,1},{9,5},{13... | collective-permute-start | bytes 255752 | tf_op jit(solution)/shard_map/ppermute | solution.py:31
  4.3 4.6 %collective-permute-start = (f32[72,296]{1,0:T(8,128)}, f32[72,296]{1,0:T(8,128)S(1)}, u32[]{:S(2)}, u32[]{:S(2)}) collective-permute-start(f32[72,296]{1,0:T(8,128)} %param.6), channel_id=1, source_target_pairs={{0,4},{4,8},{8,12},{12,16},{16,20},{20,24},{24,28},{1,5},{5,9},{9,... | collective-permute-start | bytes 255752 | tf_op jit(solution)/shard_map/ppermute | solution.py:31
  8.8 2.0 %selections.1 = (bf16[16,288,512]{2,1,0:T(8,128)(2,1)S(1)}, f32[72,128]{1,0:T(8,128)S(1)}) custom-call(s32[8]{0:T(128)} %owner_ref.1, s32[8]{0:T(128)} %group_ref.1, s32[1,16,288]{2,1,0:T(8,128)} %target_hbm.1, s32[1,16,288]{2,1,0:T(8,128)} %source_hbm.1), custom_call_target="tpu_custom_call" | custom-call | bytes 4718592 | tf_op jit(solution)/shard_map/selections/pallas_call | solution.py:112
  10.8 0.0 collective-permute-done.2
  10.8 0.9 %pad_maximum_fusion.4 = f32[144,296]{1,0:T(8,128)S(1)} fusion(f32[72,296]{1,0:T(8,128)S(1)} %collective-permute-done.2, f32[72,296]{1,0:T(8,128)} %param.6), kind=kLoop, calls=%fused_computation.4 | loop fusion | flops 42624 | bytes 340992 | tf_op jit(solution)/shard_map/concatenate | solution.py:385
  11.7 0.0 collective-permute-done.1
  11.7 0.3 collective-permute-done
  12.1 0.0 copy-start
  12.1 0.0 copy-start.1
  12.1 0.1 collective-permute-start.4
  12.2 0.5 %collective-permute-start.3 = (f32[144,296]{1,0:T(8,128)S(1)}, f32[144,296]{1,0:T(8,128)S(1)}, u32[]{:S(2)}, u32[]{:S(2)}) collective-permute-start(f32[144,296]{1,0:T(8,128)S(1)} %pad_maximum_fusion.3), channel_id=1, source_target_pairs={{0,2},{1,3},{2,0},{3,1},{4,6},{5,7},{6,4},{7,5},{8,10},{9,11},{10,... | collective-permute-start | bytes 511496 | tf_op jit(solution)/shard_map/ppermute | solution.py:27
  12.7 4.1 %split_operators.1 = (bf16[16,256,640]{2,1,0:T(8,128)(2,1)S(1)}, bf16[16,96,384]{2,1,0:T(8,128)(2,1)S(1)}) custom-call(f32[16,296,296]{2,1,0:T(8,128)} %op_hbm.1), custom_call_target="tpu_custom_call" | custom-call | bytes 5607424 | tf_op jit(solution)/shard_map/split_operators/pallas_call | solution.py:178
  16.9 0.0 collective-permute-done.4
  16.9 3.1 %collective-permute-done.3 = f32[144,296]{1,0:T(8,128)S(1)} collective-permute-done((f32[144,296]{1,0:T(8,128)S(1)}, f32[144,296]{1,0:T(8,128)S(1)}, u32[]{:S(2)}, u32[]{:S(2)}) %collective-permute-start.3) | collective-permute-done | bytes 170528 | tf_op jit(solution)/shard_map/ppermute | solution.py:27
  20.0 0.1 collective-permute-start.5
  20.2 1.7 %collective-permute-done.5 = f32[288,296]{1,0:T(8,128)S(1)} collective-permute-done((f32[288,296]{1,0:T(8,128)S(1)}, f32[288,296]{1,0:T(8,128)S(1)}, u32[]{:S(2)}, u32[]{:S(2)}) %collective-permute-start.5) | collective-permute-done | bytes 341024 | tf_op jit(solution)/shard_map/ppermute | solution.py:27
  21.9 0.1 pad_maximum_fusion.near_ref
  22.0 0.0 copy-done
  22.0 0.0 copy-done.1
  22.0 10.2 %translate.1 = (f32[288,296]{1,0:T(8,128)S(1)}, f32[288,296]{1,0:T(8,128)S(1)}) custom-call(s32[8]{0:T(128)S(1)} %copy-done, s32[8]{0:T(128)S(1)} %copy-done.1, f32[288,296]{1,0:T(8,128)S(1)} %pad_maximum_fusion.1.own_ref, f32[576,296]{1,0:T(8,128)S(1)} %pad_maximum_fusion.near_ref, bf16[16,256,640]{2,1,0:T(8,128)(2,1)S(1)} %get-tuple-element.25.weight_ref, ...), custom_call_target="tpu_custom_call" | custom-call | tf_op jit(solution)/shard_map/translate/pallas_call | solution.py:346
  32.2 0.2 collective-permute-start.6
  32.4 1.7 %collective-permute-done.6 = f32[288,296]{1,0:T(8,128)S(1)} collective-permute-done((f32[288,296]{1,0:T(8,128)S(1)}, f32[288,296]{1,0:T(8,128)S(1)}, u32[]{:S(2)}, u32[]{:S(2)}) %collective-permute-start.6) | collective-permute-done | bytes 341024 | tf_op jit(solution)/shard_map/ppermute | solution.py:27
  34.2 4.3 %collective-permute-start.7 = (f32[72,296]{1,0:T(8,128)S(1)}, f32[72,296]{1,0:T(8,128)S(1)}, u32[]{:S(2)}, u32[]{:S(2)}) collective-permute-start(f32[72,296]{1,0:T(8,128)S(1)} %get-tuple-element.31), channel_id=1, source_target_pairs={{0,4},{4,8},{8,12},{12,16},{16,20},{20,24},{24,28},{1,5},{5,9},{9,... | collective-permute-start | bytes 255752 | tf_op jit(solution)/shard_map/ppermute | solution.py:31
  38.5 1.3 %collective-permute-start.8 = (f32[72,296]{1,0:T(8,128)S(1)}, f32[72,296]{1,0:T(8,128)S(1)}, u32[]{:S(2)}, u32[]{:S(2)}) collective-permute-start(f32[72,296]{1,0:T(8,128)S(1)} %get-tuple-element.32), channel_id=1, source_target_pairs={{4,0},{8,4},{12,8},{16,12},{20,16},{24,20},{28,24},{5,1},{9,5},{13... | collective-permute-start | bytes 255752 | tf_op jit(solution)/shard_map/ppermute | solution.py:31
  39.8 0.1 fusion.1
  39.9 1.2 %collective-permute-done.7 = f32[72,296]{1,0:T(8,128)S(1)} collective-permute-done((f32[72,296]{1,0:T(8,128)S(1)}, f32[72,296]{1,0:T(8,128)S(1)}, u32[]{:S(2)}, u32[]{:S(2)}) %collective-permute-start.7) | collective-permute-done | bytes 85280 | tf_op jit(solution)/shard_map/ppermute | solution.py:31
  41.0 5.0 %collective-permute-done.8 = f32[72,296]{1,0:T(8,128)S(1)} collective-permute-done((f32[72,296]{1,0:T(8,128)S(1)}, f32[72,296]{1,0:T(8,128)S(1)}, u32[]{:S(2)}, u32[]{:S(2)}) %collective-permute-start.8) | collective-permute-done | bytes 85280 | tf_op jit(solution)/shard_map/ppermute | solution.py:31
  46.1 0.1 broadcast_select_fusion
  46.2 0.6 %collective-permute-start.9 = (f32[72,296]{1,0:T(8,128)S(1)}, f32[72,296]{1,0:T(8,128)S(1)}, u32[]{:S(2)}, u32[]{:S(2)}) collective-permute-start(f32[72,296]{1,0:T(8,128)S(1)} %broadcast_select_fusion), channel_id=1, source_target_pairs={{0,2},{1,3},{2,0},{3,1},{4,6},{5,7},{6,4},{7,5},{8,10},{9,11},{10,... | collective-permute-start | bytes 255752 | tf_op jit(solution)/shard_map/ppermute | solution.py:27
  46.8 4.2 %collective-permute-done.9 = f32[72,296]{1,0:T(8,128)S(1)} collective-permute-done((f32[72,296]{1,0:T(8,128)S(1)}, f32[72,296]{1,0:T(8,128)S(1)}, u32[]{:S(2)}, u32[]{:S(2)}) %collective-permute-start.9) | collective-permute-done | bytes 85280 | tf_op jit(solution)/shard_map/ppermute | solution.py:27
  51.0 0.7 %select_add_fusion = f32[72,296]{1,0:T(8,128)} fusion(f32[72,296]{1,0:T(8,128)S(1)} %collective-permute-done.9, pred[]{:T(512)S(6)} %lt.3, f32[72,296]{1,0:T(8,128)S(1)} %collective-permute-done.8, pred[72]{0:T(512)(128)(4,1)S(1)} %fusion.1, f32[288,296]{1,0:T(8,128)S(1)} %add.15, f32[72,296]{1,0:T(8,128)S(1)} %collective-permute-done.7), kind=kLoop, calls=%fused_computation.8 | loop fusion | flops 149184 | bytes 511561 | tf_op jit(solution)/shard_map/add | solution.py:408
  (5 shorter events, 0.1 us)
Async XLA Ops:
  0.0 10.8 %collective-permute-start.2 = (f32[72,296]{1,0:T(8,128)}, f32[72,296]{1,0:T(8,128)S(1)}, u32[]{:S(2)}, u32[]{:S(2)}) collective-permute-start(f32[72,296]{1,0:T(8,128)} %param.6), channel_id=1, source_target_pairs={{0,2},{1,3},{2,0},{3,1},{4,6},{5,7},{6,4},{7,5},{8,10},{9,11},{10,... | collective-permute-start | bytes 255752 | tf_op jit(solution)/shard_map/ppermute | solution.py:27
  3.0 8.8 %collective-permute-start.1 = (f32[72,296]{1,0:T(8,128)}, f32[72,296]{1,0:T(8,128)S(1)}, u32[]{:S(2)}, u32[]{:S(2)}) collective-permute-start(f32[72,296]{1,0:T(8,128)} %param.6), channel_id=1, source_target_pairs={{4,0},{8,4},{12,8},{16,12},{20,16},{24,20},{28,24},{5,1},{9,5},{13... | collective-permute-start | bytes 255752 | tf_op jit(solution)/shard_map/ppermute | solution.py:31
  4.3 7.8 %collective-permute-start = (f32[72,296]{1,0:T(8,128)}, f32[72,296]{1,0:T(8,128)S(1)}, u32[]{:S(2)}, u32[]{:S(2)}) collective-permute-start(f32[72,296]{1,0:T(8,128)} %param.6), channel_id=1, source_target_pairs={{0,4},{4,8},{8,12},{12,16},{16,20},{20,24},{24,28},{1,5},{5,9},{9,... | collective-permute-start | bytes 255752 | tf_op jit(solution)/shard_map/ppermute | solution.py:31
  12.1 9.9 %copy-start = (s32[8]{0:T(128)S(1)}, s32[8]{0:T(128)}, u32[]{:S(2)}) copy-start(s32[8]{0:T(128)} %owner_ref.1) | copy-start | bytes 100
  12.1 9.9 %copy-start.1 = (s32[8]{0:T(128)S(1)}, s32[8]{0:T(128)}, u32[]{:S(2)}) copy-start(s32[8]{0:T(128)} %group_ref.1) | copy-start | bytes 100
  12.1 4.8 %collective-permute-start.4 = (f32[144,296]{1,0:T(8,128)S(1)}, f32[144,296]{1,0:T(8,128)S(1)}, u32[]{:S(2)}, u32[]{:S(2)}) collective-permute-start(f32[144,296]{1,0:T(8,128)S(1)} %pad_maximum_fusion.4), channel_id=1, source_target_pairs={{0,1},{1,0},{2,3},{3,2},{4,5},{5,4},{6,7},{7,6},{8,9},{9,8},{10,11... | collective-permute-start | bytes 511496 | tf_op jit(solution)/shard_map/ppermute | solution.py:27
  12.2 7.8 %collective-permute-start.3 = (f32[144,296]{1,0:T(8,128)S(1)}, f32[144,296]{1,0:T(8,128)S(1)}, u32[]{:S(2)}, u32[]{:S(2)}) collective-permute-start(f32[144,296]{1,0:T(8,128)S(1)} %pad_maximum_fusion.3), channel_id=1, source_target_pairs={{0,2},{1,3},{2,0},{3,1},{4,6},{5,7},{6,4},{7,5},{8,10},{9,11},{10,... | collective-permute-start | bytes 511496 | tf_op jit(solution)/shard_map/ppermute | solution.py:27
  20.0 1.9 %collective-permute-start.5 = (f32[288,296]{1,0:T(8,128)S(1)}, f32[288,296]{1,0:T(8,128)S(1)}, u32[]{:S(2)}, u32[]{:S(2)}) collective-permute-start(f32[288,296]{1,0:T(8,128)S(1)} %pad_maximum_fusion.2), channel_id=1, source_target_pairs={{0,1},{1,0},{2,3},{3,2},{4,5},{5,4},{6,7},{7,6},{8,9},{9,8},{10,11... | collective-permute-start | bytes 1022984 | tf_op jit(solution)/shard_map/ppermute | solution.py:27
  32.2 1.9 %collective-permute-start.6 = (f32[288,296]{1,0:T(8,128)S(1)}, f32[288,296]{1,0:T(8,128)S(1)}, u32[]{:S(2)}, u32[]{:S(2)}) collective-permute-start(f32[288,296]{1,0:T(8,128)S(1)} %get-tuple-element.29), channel_id=1, source_target_pairs={{0,1},{1,0},{2,3},{3,2},{4,5},{5,4},{6,7},{7,6},{8,9},{9,8},{10,11... | collective-permute-start | bytes 1022984 | tf_op jit(solution)/shard_map/ppermute | solution.py:27
  34.2 6.9 %collective-permute-start.7 = (f32[72,296]{1,0:T(8,128)S(1)}, f32[72,296]{1,0:T(8,128)S(1)}, u32[]{:S(2)}, u32[]{:S(2)}) collective-permute-start(f32[72,296]{1,0:T(8,128)S(1)} %get-tuple-element.31), channel_id=1, source_target_pairs={{0,4},{4,8},{8,12},{12,16},{16,20},{20,24},{24,28},{1,5},{5,9},{9,... | collective-permute-start | bytes 255752 | tf_op jit(solution)/shard_map/ppermute | solution.py:31
  38.5 7.6 %collective-permute-start.8 = (f32[72,296]{1,0:T(8,128)S(1)}, f32[72,296]{1,0:T(8,128)S(1)}, u32[]{:S(2)}, u32[]{:S(2)}) collective-permute-start(f32[72,296]{1,0:T(8,128)S(1)} %get-tuple-element.32), channel_id=1, source_target_pairs={{4,0},{8,4},{12,8},{16,12},{20,16},{24,20},{28,24},{5,1},{9,5},{13... | collective-permute-start | bytes 255752 | tf_op jit(solution)/shard_map/ppermute | solution.py:31
  46.2 4.8 %collective-permute-start.9 = (f32[72,296]{1,0:T(8,128)S(1)}, f32[72,296]{1,0:T(8,128)S(1)}, u32[]{:S(2)}, u32[]{:S(2)}) collective-permute-start(f32[72,296]{1,0:T(8,128)S(1)} %broadcast_select_fusion), channel_id=1, source_target_pairs={{0,2},{1,3},{2,0},{3,1},{4,6},{5,7},{6,4},{7,5},{8,10},{9,11},{10,... | collective-permute-start | bytes 255752 | tf_op jit(solution)/shard_map/ppermute | solution.py:27
